TPU v7x, 32 devices: a whole 2x2x4 slice. The times are simulated.
32 devices in a mesh: sample: 16 (over z, y, core), gene: 2 (over x).
Axes of the slice: x: 2, y: 2, z: 4, core: 2. Of those that a mesh axis runs over, the one named last changes fastest.
Arguments:
- block_values: bfloat16 [2048, 128, 128], P(('sample', 'gene')), may hold values from -0.1875 to 0.1875
- block_coords: int32 [2048, 2], P(('sample', 'gene')), may hold values from 0 to 127, as said below
- block_counts: int32 [32], P(('sample', 'gene')), may hold values from 13 to 64, as said below
- random_cols: bfloat16 [32768, 256], P(('gene', 'sample')), may hold values from -6 to 6
Outputs:
- basis: float32 [16384, 256], P(('sample', 'gene'))
- factor: float32 [256, 256], replicated
Inputs may be any that keep to these rules, and one draw needn't show every extreme that they name: `block_coords`: column 0 is a row block 0 to 7, column 1 a column block 0 to 127; the pairs of one device's slots are all distinct. `block_counts`: some devices use all 64 slots in every draw.
All inputs are finite; a program needn't handle non-finite values.
Results may differ from a plain program's by a relative error of at most 0.0027.
Values may be sent and summed in bfloat16 or wider, within the bound.
No kernel may reach another device: no remote copies, remote signals or barrier semaphores. Data moves between devices by JAX's collectives and lax.ppermute only.
A program may use at most 128 MiB of HBM per device.

v0:
```python
import jax
import jax.numpy as jnp
from jax import lax
from jax.sharding import PartitionSpec as P

RANK = 256
BLOCK = 128
RB_DEV = 8


def forward_product(block_values, block_coords, alive_mask, right_full):
    right_blocks = right_full.reshape(-1, BLOCK, RANK)
    slot_count = block_values.shape[0]
    per_turn = min(32, slot_count)
    summed = jnp.zeros((RB_DEV, BLOCK, RANK), jnp.float32)
    for offset in range(0, slot_count, per_turn):
        finish = min(offset + per_turn, slot_count)
        picked = jnp.take(right_blocks, block_coords[offset:finish, 1], axis=0)
        products = jnp.einsum(
            "nij,njk->nik", block_values[offset:finish], picked, preferred_element_type=jnp.float32
        )
        weighted = products * alive_mask[offset:finish][:, None, None]
        summed = summed.at[block_coords[offset:finish, 0]].add(weighted)
    return summed.reshape(RB_DEV * BLOCK, RANK)


def backward_product(block_values, block_coords, alive_mask, left_rows, span_blocks):
    left_blocks = left_rows.reshape(RB_DEV, BLOCK, RANK)
    slot_count = block_values.shape[0]
    per_turn = min(32, slot_count)
    summed = jnp.zeros((span_blocks, BLOCK, RANK), jnp.float32)
    for offset in range(0, slot_count, per_turn):
        finish = min(offset + per_turn, slot_count)
        picked = jnp.take(left_blocks, block_coords[offset:finish, 0], axis=0)
        products = jnp.einsum(
            "nij,nik->njk", block_values[offset:finish], picked, preferred_element_type=jnp.float32
        )
        weighted = products * alive_mask[offset:finish][:, None, None]
        summed = summed.at[block_coords[offset:finish, 1]].add(weighted)
    return summed.reshape(span_blocks * BLOCK, RANK)


def gram_of(rows_block):
    return jnp.dot(
        rows_block.T,
        rows_block,
        precision=lax.Precision.HIGHEST,
        preferred_element_type=jnp.float32,
    )


def solve_rows(lower, rows_block):
    return jax.scipy.linalg.solve_triangular(lower, rows_block.T, lower=True).T


def orthonormal(partial_value, cells):
    gene_count = lax.axis_size("gene")
    share = partial_value.shape[0] // gene_count
    summed = lax.psum(partial_value, "gene")
    gram = lax.psum(gram_of(summed), "sample")
    lower = jnp.linalg.cholesky(gram / cells)
    full_basis = solve_rows(lower, summed)
    basis = lax.dynamic_slice_in_dim(full_basis, lax.axis_index("gene") * share, share, 0)
    whole = full_basis.astype(jnp.bfloat16)
    return (basis, lower, whole)


def local(block_values, block_coords, block_counts, random_cols):
    random_full = lax.all_gather(random_cols, "sample", axis=0, tiled=True)
    span_blocks = random_full.shape[0] // BLOCK
    slot_count = block_values.shape[0]
    alive_mask = (jnp.arange(slot_count, dtype=jnp.int32) < block_counts[0]).astype(jnp.float32)
    cells = RB_DEV * BLOCK * lax.axis_size("sample")
    sketch = forward_product(block_values, block_coords, alive_mask, random_full)
    first_basis, first_lower, basis_whole = orthonormal(sketch, cells)
    loading_part = backward_product(
        block_values, block_coords, alive_mask, basis_whole, span_blocks
    )
    loading_mine = lax.psum_scatter(loading_part, "sample", scatter_dimension=0, tiled=True).astype(
        jnp.bfloat16
    )
    loading_full = lax.all_gather(loading_mine, "sample", axis=0, tiled=True)
    second_sketch = forward_product(block_values, block_coords, alive_mask, loading_full)
    basis, second_lower, unused_whole = orthonormal(second_sketch, cells)
    return (basis, second_lower.T)


def solution(mesh):
    return jax.shard_map(
        local,
        mesh=mesh,
        in_specs=(
            P(("sample", "gene"), None, None),
            P(("sample", "gene"), None),
            P(("sample", "gene")),
            P(("gene", "sample"), None),
        ),
        out_specs=(P(("sample", "gene"), None), P()),
        check_vma=False,
    )
```

profile of v0, /device:TPU:0, one launch (start us, length us, event | category | flops | bytes accessed | tf_op | source)
XLA Modules:
  0.0 911.7 jit_solution(34158779275634026)
XLA Ops:
  8.6 1.4 compare_and_fusion.1
  10.1 1.5 fusion.53
  11.6 75.6 %all-gather.3.cloned.1.call-done = bf16[16384,256]{1,0:T(8,128)(2,1)} async-done(((bf16[1024,256]{1,0:T(8,128)(2,1)}), bf16[16384,256]{1,0:T(8,128)(2,1)}) %all-gather.3.cloned.1.call-update) | async-done | bytes 8388624 | tf_op jit(solution)/shard_map/all_gather | solution.py:69
  87.2 5.6 gather_fusion
  92.8 4.6 multiply_bitcast_fusion.5
  97.3 5.6 copy.19
  102.9 5.4 gather_fusion.1
  108.3 4.5 multiply_bitcast_fusion.4
  112.9 5.6 copy.21
  118.6 6.4 scatter_fusion
  125.0 6.5 scatter_fusion.1
  131.5 1.0 copy-done.1
  132.6 38.8 %all-reduce.6.cloned.1.call-done = f32[1024,256]{1,0:T(8,128)} async-done(((f32[1024,256]{1,0:T(8,128)}), f32[1024,256]{1,0:T(8,128)}) %all-reduce.6.cloned.1.call-update) | async-done | bytes 1048592 | tf_op jit(solution)/shard_map/psum | solution.py:59
  171.4 4.1 fusion.63
  176.9 88.5 %all-reduce.8.cloned.1.call-done = f32[256,256]{0,1:T(8,128)} async-done(((f32[256,256]{0,1:T(8,128)}), f32[256,256]{0,1:T(8,128)}) %all-reduce.8.cloned.1.call-update) | async-done | bytes 262160 | tf_op jit(solution)/shard_map/psum | solution.py:60
  265.4 1.7 broadcast_multiply_fusion.1
  267.0 1.2 copy.23
  269.9 11.7 %cholesky.130 = f32[128,128]{1,0:T(8,128)S(1)} custom-call(f32[128,128]{1,0:T(8,128)S(1)} %cholesky.194), custom_call_target="Cholesky" | custom-call | tf_op jit(solution)/shard_map/jit(cholesky)/cholesky | solution.py:61
  282.2 9.8 %custom-call.13 = f32[1,128,128]{1,2,0:T(8,128)S(1)} custom-call(f32[1,128,128]{2,1,0:T(8,128)S(1)} %get-tuple-element.63), custom_call_target="InvertDiagBlocksLowerTriangular" | custom-call | tf_op jit(solution)/shard_map/jit(cholesky)/cholesky | solution.py:61
  292.0 1.0 constant_dynamic-update-slice_fusion.1
  293.1 1.1 convolution_subtract_fusion.3
  294.2 11.7 %cholesky.147 = f32[128,128]{1,0:T(8,128)S(1)} custom-call(f32[128,128]{1,0:T(8,128)S(1)} %convolution_subtract_fusion.3), custom_call_target="Cholesky" | custom-call | tf_op jit(solution)/shard_map/jit(cholesky)/cholesky | solution.py:61
  306.6 1.3 compare_reduce_fusion.3
  310.1 1.2 triangular_solve.75
  311.3 17.6 %while.4 = (s32[]{:T(128)}, f32[256,256]{1,0:T(8,128)S(1)}, s32[2,2]{1,0:T(2,128)}, f32[2,128,128]{2,1,0:T(8,128)S(1)}, s32[]{:T(128)}) while((s32[]{:T(128)}, f32[256,256]{1,0:T(8,128)S(1)}, s32[2,2]{1,0:T(2,128)}, f32[2,128,128]{2,1,0:T(8,128)S(1)}, s32[]{:T(128)}) %tuple.67), condition=%wide.while_cond, body=%wide.while_body.sunk | while | flops 2 | bytes 131181 | solution.py:53
  324.9 1.4 bitcast_dynamic-update-slice_fusion.4
  327.5 1.4 bitcast_dynamic-update-slice_fusion.4
  328.9 20.3 %custom-call.14 = f32[2,128,128]{1,2,0:T(8,128)} custom-call(f32[2,128,128]{2,1,0:T(8,128)S(1)} %get-tuple-element.20), custom_call_target="InvertDiagBlocksLowerTriangular" | custom-call | tf_op jit(solution)/shard_map/jit(_solve_triangular)/triangular_solve | solution.py:53
  349.2 1.6 fusion.29
  350.7 1.0 convolution_subtract_fusion.1
  352.7 2.1 gather_fusion.2
  354.8 4.5 multiply_bitcast_fusion.3
  359.3 5.6 copy.26
  364.9 2.3 gather_fusion.3
  367.2 4.5 multiply_bitcast_fusion.2
  371.7 5.6 copy.29
  377.4 7.8 broadcast_in_dim.21
  385.2 10.1 %scatter_fusion.2 = f32[128,128,256]{2,1,0:T(8,128)} fusion(f32[128,128,256]{2,1,0:T(8,128)} %broadcast_in_dim.21, s32[32]{0:T(128)S(1)} %copy-done.19, f32[32,128,256]{2,1,0:T(8,128)} %copy.26), kind=kCustom, calls=%fused_computation.8 | custom fusion | flops 1048576 | bytes 12583040 | tf_op jit(solution)/shard_map/scatter-add | solution.py:39
  395.2 10.1 %scatter_fusion.3 = f32[128,128,256]{2,1,0:T(8,128)} fusion(f32[128,128,256]{2,1,0:T(8,128)} %scatter_fusion.2, s32[32]{0:T(128)S(1)} %copy-done.18, f32[32,128,256]{2,1,0:T(8,128)} %copy.29), kind=kCustom, calls=%fused_computation.9 | custom fusion | flops 1048576 | bytes 12583040 | tf_op jit(solution)/shard_map/scatter-add | solution.py:39
  405.5 178.0 %reduce-scatter.2.cloned.1.call-done = f32[1024,256]{1,0:T(8,128)} async-done(((f32[16384,256]{1,0:T(8,128)}), f32[1024,256]{1,0:T(8,128)}) %reduce-scatter.2.cloned.1.call-update) | async-done | bytes 1048592 | tf_op jit(solution)/shard_map/reduce_scatter | solution.py:79
  583.5 2.1 convert_element_type.15
  585.6 73.9 %all-gather.5.cloned.1.call-done = bf16[16384,256]{1,0:T(8,128)(2,1)} async-done(((bf16[1024,256]{1,0:T(8,128)(2,1)}), bf16[16384,256]{1,0:T(8,128)(2,1)}) %all-gather.5.cloned.1.call-update) | async-done | bytes 8388624 | tf_op jit(solution)/shard_map/all_gather | solution.py:82
  659.5 5.4 gather_fusion.4
  665.0 5.4 gather_fusion.5
  670.4 4.6 multiply_bitcast_fusion.1
  674.9 5.6 copy.31
  680.5 4.6 multiply_bitcast_fusion
  685.1 5.6 copy.33
  690.8 6.4 scatter_fusion.4
  697.3 6.5 scatter_fusion.5
  703.8 1.0 copy-done
  705.1 38.6 %all-reduce.10.cloned.1.call-done = f32[1024,256]{1,0:T(8,128)} async-done(((f32[1024,256]{1,0:T(8,128)}), f32[1024,256]{1,0:T(8,128)}) %all-reduce.10.cloned.1.call-update) | async-done | bytes 1048592 | tf_op jit(solution)/shard_map/psum | solution.py:59
  743.6 4.1 fusion.64
  747.7 89.9 %all-reduce.12.cloned.1.call-done = f32[256,256]{0,1:T(8,128)} async-done(((f32[256,256]{0,1:T(8,128)}), f32[256,256]{0,1:T(8,128)}) %all-reduce.12.cloned.1.call-update) | async-done | bytes 262160 | tf_op jit(solution)/shard_map/psum | solution.py:60
  838.7 1.1 fusion.31
  839.8 11.7 %cholesky.164 = f32[128,128]{1,0:T(8,128)S(1)} custom-call(f32[128,128]{1,0:T(8,128)S(1)} %cholesky.197), custom_call_target="Cholesky" | custom-call | tf_op jit(solution)/shard_map/jit(cholesky)/cholesky | solution.py:61
  851.6 9.8 %custom-call.15 = f32[1,128,128]{1,2,0:T(8,128)S(1)} custom-call(f32[1,128,128]{2,1,0:T(8,128)S(1)} %get-tuple-element.59), custom_call_target="InvertDiagBlocksLowerTriangular" | custom-call | tf_op jit(solution)/shard_map/jit(cholesky)/cholesky | solution.py:61
  861.9 11.7 %cholesky.181 = f32[128,128]{1,0:T(8,128)S(1)} custom-call(f32[128,128]{1,0:T(8,128)S(1)} %convolution_subtract_fusion.2), custom_call_target="Cholesky" | custom-call | tf_op jit(solution)/shard_map/jit(cholesky)/cholesky | solution.py:61
  876.5 4.0 while.5
  877.1 1.4 bitcast_dynamic-update-slice_fusion.5
  879.1 1.4 bitcast_dynamic-update-slice_fusion.5
  880.5 19.7 %custom-call.16 = f32[2,128,128]{1,2,0:T(8,128)S(1)} custom-call(f32[2,128,128]{2,1,0:T(8,128)S(1)} %get-tuple-element.21), custom_call_target="InvertDiagBlocksLowerTriangular" | custom-call | tf_op jit(solution)/shard_map/jit(_solve_triangular)/triangular_solve | solution.py:53
  900.8 1.0 convolution_subtract_fusion
  902.5 1.0 copy.36
  (96 shorter events, 16.8 us)
Async XLA Ops:
  7.2 80.0 %all-gather.3.cloned.1.call-start = ((), (), s32[]{:S(2)}) async-start(), calls=%async_computation.1 | async-start | bytes 8912896 | tf_op jit(solution)/shard_map/all_gather | solution.py:69
  7.9 163.5 %all-reduce.6.cloned.1.call-start = ((), (), s32[]{:S(2)}) async-start(), calls=%async_computation.2 | async-start | bytes 2097152 | tf_op jit(solution)/shard_map/psum | solution.py:59
  10.0 82.8 %copy-start.10 = (pred[32]{0:T(512)(128)(4,1)}, pred[32]{0:T(512)(128)(4,1)S(1)}, u32[]{:S(2)}) copy-start(pred[32]{0:T(512)(128)(4,1)S(1)} %get-tuple-element.64) | copy-start | bytes 100
  10.0 98.3 %copy-start.8 = (pred[32]{0:T(512)(128)(4,1)}, pred[32]{0:T(512)(128)(4,1)S(1)}, u32[]{:S(2)}) copy-start(pred[32]{0:T(512)(128)(4,1)S(1)} %get-tuple-element.68) | copy-start | bytes 100
  11.6 107.0 %copy-start.14 = (s32[32]{0:T(128)}, s32[32]{0:T(128)S(1)}, u32[]{:S(2)}) copy-start(s32[32]{0:T(128)S(1)} %get-tuple-element.71) | copy-start | bytes 388
  11.6 113.5 %copy-start.12 = (s32[32]{0:T(128)}, s32[32]{0:T(128)S(1)}, u32[]{:S(2)}) copy-start(s32[32]{0:T(128)S(1)} %get-tuple-element.73) | copy-start | bytes 388
  87.2 5.6 copy-start.2
  131.5 1.0 copy-start.1
  132.6 132.8 %all-reduce.8.cloned.1.call-start = ((), (), s32[]{:S(2)}) async-start(), calls=%async_computation.3 | async-start | bytes 524288 | tf_op jit(solution)/shard_map/psum | solution.py:60
  175.5 408.0 %reduce-scatter.2.cloned.1.call-start = ((), (), s32[]{:S(2)}) async-start(), calls=%async_computation.4 | async-start | bytes 17825792 | tf_op jit(solution)/shard_map/reduce_scatter | solution.py:79
  267.0 82.1 %copy-start.4 = (f32[1024,256]{1,0:T(8,128)S(1)}, f32[1024,256]{1,0:T(8,128)}, u32[]{:S(2)}) copy-start(f32[1024,256]{1,0:T(8,128)} %all-reduce.6.cloned.1.call-done) | copy-start | bytes 3145732
  269.2 0.7 copy-start.6
  306.0 3.1 copy-start.5
  349.2 2.6 copy-start.7
  352.7 2.1 copy-start.17
  364.9 2.3 copy-start.16
  377.3 7.8 copy-start.19
  385.2 10.1 %copy-start.18 = (s32[32]{0:T(128)S(1)}, s32[32]{0:T(128)}, u32[]{:S(2)}) copy-start(s32[32]{0:T(128)} %get-tuple-element.70) | copy-start | bytes 388
  405.4 254.1 %all-gather.5.cloned.1.call-start = ((), (), s32[]{:S(2)}) async-start(), calls=%async_computation.5 | async-start | bytes 8912896 | tf_op jit(solution)/shard_map/all_gather | solution.py:82
  585.6 158.1 %all-reduce.10.cloned.1.call-start = ((), (), s32[]{:S(2)}) async-start(), calls=%async_computation.6 | async-start | bytes 2097152 | tf_op jit(solution)/shard_map/psum | solution.py:59
  665.0 5.4 copy-start.11
  674.9 5.6 copy-start.9
  685.1 5.7 copy-start.15
  690.8 6.5 copy-start.13
  703.7 1.0 copy-start
  704.8 132.8 %all-reduce.12.cloned.1.call-start = ((), (), s32[]{:S(2)}) async-start(), calls=%async_computation.7 | async-start | bytes 524288 | tf_op jit(solution)/shard_map/psum | solution.py:60
  747.7 128.8 %copy-start.20 = (s32[2,2]{1,0:T(2,128)S(1)}, s32[2,2]{1,0:T(2,128)}, u32[]{:S(2)}) copy-start(s32[2,2]{1,0:T(2,128)} %get-tuple-element.202) | copy-start | bytes 52
  838.6 61.6 %copy-start.3 = (f32[1024,256]{1,0:T(8,128)S(1)}, f32[1024,256]{1,0:T(8,128)}, u32[]{:S(2)}) copy-start(f32[1024,256]{1,0:T(8,128)} %all-reduce.10.cloned.1.call-done) | copy-start | bytes 3145732
Sparse Core Ops, SparseCore 0:
  10.1 77.0 all-gather.2
  132.7 38.6 all-reduce.5
  175.6 89.7 all-reduce.7
  405.5 177.9 reduce-scatter.1
  586.1 73.3 all-gather.4
  704.9 38.6 all-reduce.9
  747.8 89.7 all-reduce.11
where the time goes:
time: 920 us; the launch traced here: 912 us
  waiting for transfers between devices  584 us (63%)
  other arithmetic  168 us (18%)
  local copies, waits for them, and re-layouts  84.3 us (9%)
  matrix products  43.6 us (5%)
  between operations  18.1 us (2%)
  loops' own time  12.4 us (1%)
    psum x2, waiting for transfers between devices, orthonormal(): gram = lax.psum(gram_of(summed), 'sample')  178 us
    reduce_scatter x1, waiting for transfers between devices, local(): lax.psum_scatter(loading_part, 'sample', scatter_dimension=0, tiled=True)  178 us
    psum x2, waiting for transfers between devices, orthonormal(): summed = lax.psum(partial_value, 'gene')  77.4 us
    all_gather x1, waiting for transfers between devices, local(): random_full = lax.all_gather(random_cols, 'sample', axis=0, tiled=True)  75.6 us
    all_gather x1, waiting for transfers between devices, local(): loading_full = lax.all_gather(loading_mine, 'sample', axis=0, tiled=True)  73.9 us
    another operation x14, other arithmetic, orthonormal(): lower = jnp.linalg.cholesky(gram / cells)  70.6 us
    another operation x4, other arithmetic, solve_rows(): return jax.scipy.linalg.solve_triangular(lower, rows_block.T, lower=True).T  41.4 us
    scatter-add x4, other arithmetic, forward_product(): summed = summed.at[block_coords[offset:finish, 0]].add(weighted)  25.8 us
  transfers between devices with their start and end apart: 7, of which 7 were waited for; matrix products, arithmetic and copies ran while one was open for 0% of the time, Pallas kernels for 0%

commit v1 on v0

v1 whole, which is shorter than its diff:
```python
import functools

import jax
import jax.numpy as jnp
from jax import lax
from jax.experimental import pallas as pl
from jax.experimental.pallas import tpu as pltpu
from jax.sharding import PartitionSpec as P

RANK = 256
BLOCK = 128
RB_DEV = 8
HALF = RANK // 2
PANEL = 16
UNROLL = 8
F32, BF16 = jnp.float32, jnp.bfloat16
ANY = pl.BlockSpec(memory_space=pl.ANY)
SMEM = pl.BlockSpec(memory_space=pltpu.SMEM)
VMEM = pl.BlockSpec(memory_space=pltpu.VMEM)


def split3(value):
    high = value.astype(BF16)
    rest = value - high.astype(F32)
    middle = rest.astype(BF16)
    return high, middle, (rest - middle.astype(F32)).astype(BF16)


def factor_kernel(scale, gram_ref, upper_ref, inverse_ref, work):
    n = gram_ref.shape[0]
    row = lax.broadcasted_iota(jnp.int32, (n, n), 0)
    col = lax.broadcasted_iota(jnp.int32, (n, n), 1)
    work[:, :n] = gram_ref[...] * scale
    work[:, n:] = (row == col).astype(F32)
    sub = lax.broadcasted_iota(jnp.int32, (PANEL, 1), 0)
    lane = lax.broadcasted_iota(jnp.int32, (PANEL, n), 1)
    wide = 2 * n // BLOCK

    def panel(p, carry):
        start = pl.multiple_of(p * PANEL, PANEL)
        rows = work[pl.ds(start, PANEL), :]
        rolled = pltpu.roll(rows[:, :n], n - start, axis=1)
        cols = [jnp.broadcast_to(rolled[:, j : j + 1], (PANEL, BLOCK)) for j in range(PANEL)]
        for k in range(PANEL):
            pivot = jnp.broadcast_to(cols[k][k : k + 1, :], (PANEL, BLOCK))
            inv = lax.rsqrt(pivot)
            inv = inv * (1.5 - 0.5 * pivot * inv * inv)
            lower = cols[k] * inv
            below = jnp.where(sub > k, lower, 0.0)
            upper = jnp.broadcast_to(rows[k : k + 1, :], (PANEL, 2 * n)) * jnp.concatenate([inv] * wide, axis=1)
            rows = jnp.where(sub == k, upper, rows - jnp.concatenate([below] * wide, axis=1) * upper)
            for j in range(k + 1, PANEL):
                cols[j] = cols[j] - below * jnp.broadcast_to(lower[j : j + 1, :], (PANEL, BLOCK))
        work[pl.ds(start, PANEL), :] = rows
        w1, w2, w3 = split3(jnp.where(lane >= start + PANEL, rows[:, :n], 0.0))
        b1, b2, b3 = split3(rows)
        left = jnp.concatenate([w1, w1, w2, w2, w1, w3], axis=0)
        right = jnp.concatenate([b1, b2, b1, b2, b3, b1], axis=0)
        work[...] = work[...] - lax.dot_general(
            left, right, (((0,), (0,)), ((), ())), preferred_element_type=F32
        )
        return carry

    lax.fori_loop(0, n // PANEL, panel, 0)
    upper_ref[...] = jnp.where(col >= row, work[:, :n], 0.0)
    inverse_ref[...] = jnp.where(col <= row, work[:, n:], 0.0)


def factor(gram, cells):
    n = gram.shape[0]
    return pl.pallas_call(
        functools.partial(factor_kernel, 1.0 / cells),
        out_shape=[jax.ShapeDtypeStruct((n, n), F32)] * 2,
        in_specs=[VMEM],
        out_specs=[VMEM] * 2,
        scratch_shapes=[pltpu.VMEM((n, 2 * n), F32)],
        name="factor",
    )(gram)


def gram_of(rows_block):
    return jnp.dot(rows_block.T, rows_block, precision=lax.Precision.HIGHEST, preferred_element_type=F32)


class Grid:
    def __init__(self, n_sample):
        self.n, self.nz = n_sample, n_sample // 4
        self.core = [(s, s ^ 1) for s in range(n_sample)]
        self.swap = [(0, 1), (1, 0)]

    def z_of(self, s):
        return s // 4

    def along_y(self, keep):
        return [(s, s ^ 2) for s in range(self.n) if keep(self.z_of(s))]

    def up(self, keep):
        return [(s, s + 4) for s in range(self.n - 4) if keep(self.z_of(s))]

    def down(self, keep):
        return [(s, s - 4) for s in range(4, self.n) if keep(self.z_of(s))]


def gather_chips(grid, mine):
    nz = grid.nz
    move = functools.partial(lax.ppermute, axis_name="sample")
    found = [(0, 0, mine), (0, 1, move(mine, perm=grid.along_y(lambda z: True)))]
    rising = falling = mine
    for d in range(1, nz):
        rising = move(rising, perm=grid.up(lambda z: z >= d - 1))
        falling = move(falling, perm=grid.down(lambda z: z <= nz - d))
        found += [(-d, 0, rising), (d, 0, falling)]
        found += [
            (-d, 1, move(rising, perm=grid.along_y(lambda z: z >= d))),
            (d, 1, move(falling, perm=grid.along_y(lambda z: z <= nz - 1 - d))),
        ]
    return found


def position():
    s = lax.axis_index("sample")
    return s // 4, (s // 2) % 2, s % 2


def load_values(own_hbm, other_hbm, values, sems):
    slots = own_hbm.shape[0]
    copies = [
        pltpu.make_async_copy(own_hbm, values.at[pl.ds(0, slots)], sems.at[0]),
        pltpu.make_async_copy(other_hbm, values.at[pl.ds(slots, slots)], sems.at[1]),
    ]
    for copy in copies:
        copy.start()
    return copies


def forward_kernel(nz, where, flip, transposed, own_code, other_code, own_hbm, other_hbm, *refs):
    chunks = refs[: len(where)]
    keep_hbm, send_hbm, values, right, total, value_sems, chunk_sems, out_sems = refs[len(where) :]
    z, y, core = position()
    g = lax.axis_index("gene")
    slots = own_hbm.shape[0]
    per = chunks[0].shape[0]
    copies = load_values(own_hbm, other_hbm, values, value_sems)
    inside = []
    for i, (dz, dy) in enumerate(where):
        chip = (z + dz) * 2 + (y + dy) % 2
        valid = jnp.logical_and(z + dz >= 0, z + dz < nz)
        inside.append((valid, i, jnp.where(valid, chip, 0)))
    for valid, i, chip in inside:

        @pl.when(valid)
        def _():
            pltpu.make_async_copy(chunks[i], right.at[pl.ds(chip * per, per)], chunk_sems.at[i]).start()

    trash = 2 * RB_DEV
    total[...] = jnp.zeros_like(total)
    for copy in copies:
        copy.wait()
    for valid, i, chip in inside:

        @pl.when(valid)
        def _():
            pltpu.make_async_copy(chunks[i], right.at[pl.ds(chip * per, per)], chunk_sems.at[i]).wait()

    flipped = core * (per // 2) if flip else 0
    dims = (((1,), (1 if transposed else 0,)), ((), ()))
    for h, codes in enumerate((own_code, other_code)):

        def turn(t, carry):
            spots, terms = [], []
            for u in range(UNROLL):
                code = codes[t * UNROLL + u]
                r = code >> 16
                spots.append(jnp.where(r >= RB_DEV, trash, r + h * RB_DEV))
                c = (code & 0xFFFF) ^ flipped
                terms.append(
                    lax.dot_general(values[h * slots + t * UNROLL + u], right[c], dims, preferred_element_type=F32)
                )
            for spot, term in zip(spots, terms):
                total[spot] += term
            return carry

        lax.fori_loop(0, slots // UNROLL, turn, 0)
    quarter = RB_DEV // 2
    outs = []
    for h in range(2):
        for k, (out, gene) in enumerate(((keep_hbm, g), (send_hbm, 1 - g))):
            outs.append(
                pltpu.make_async_copy(
                    total.at[pl.ds(h * RB_DEV + gene * quarter, quarter)], out.at[h], out_sems.at[2 * h + k]
                )
            )
    for copy in outs:
        copy.start()
    for copy in outs:
        copy.wait()


def forward(grid, codes, values, found, flip, transposed):
    slots = values[0].shape[0]
    per = found[0][2].shape[0]
    quarter = RB_DEV // 2
    half = jax.ShapeDtypeStruct((2, quarter, BLOCK, HALF), F32)
    return pl.pallas_call(
        functools.partial(forward_kernel, grid.nz, [spot[:2] for spot in found], flip, transposed),
        out_shape=[half, half],
        in_specs=[SMEM, SMEM, ANY, ANY] + [ANY] * len(found),
        out_specs=[ANY, ANY],
        scratch_shapes=[
            pltpu.VMEM((2 * slots, BLOCK, BLOCK), BF16),
            pltpu.VMEM((2 * grid.nz * per, BLOCK, BLOCK), BF16),
            pltpu.VMEM((2 * RB_DEV + 1, BLOCK, HALF), F32),
            pltpu.SemaphoreType.DMA((2,)),
            pltpu.SemaphoreType.DMA((len(found),)),
            pltpu.SemaphoreType.DMA((4,)),
        ],
        name="forward",
    )(*codes, *values, *[chunk for _, _, chunk in found])


def backward_kernel(nz, where, own_code, other_code, own_hbm, other_hbm, near_hbm, far_hbm, *refs):
    keeps, sends = refs[: len(where)], refs[len(where) : 2 * len(where)]
    values, left, total, staged, value_sems, left_sems, keep_sems, send_sems = refs[2 * len(where) :]
    z, y, _ = position()
    g = lax.axis_index("gene")
    slots = own_hbm.shape[0]
    per = keeps[0].shape[0]
    trash = 2 * nz * per
    quarter = RB_DEV // 2
    copies = load_values(own_hbm, other_hbm, values, value_sems)
    for h in range(2):
        for k, (source, gene) in enumerate(((near_hbm, g), (far_hbm, 1 - g))):
            for j in range(quarter):
                copies.append(
                    pltpu.make_async_copy(
                        source.at[h, :, pl.ds(j * BLOCK, BLOCK)],
                        left.at[h * RB_DEV + gene * quarter + j],
                        left_sems.at[(2 * h + k) * quarter + j],
                    )
                )
    for copy in copies[2:]:
        copy.start()

    def clear(i, carry):
        total[pl.ds(i * 16, 16)] = jnp.zeros((16, HALF, BLOCK), F32)
        return carry

    lax.fori_loop(0, trash // 16, clear, 0)
    for copy in copies:
        copy.wait()
    for h, codes in enumerate((own_code, other_code)):

        def turn(t, carry):
            spots, terms = [], []
            for u in range(UNROLL):
                code = codes[t * UNROLL + u]
                r = code >> 16
                spots.append(jnp.where(r >= RB_DEV, trash, code & 0xFFFF))
                terms.append(
                    jnp.dot(
                        left[h * RB_DEV + (r & (RB_DEV - 1))],
                        values[h * slots + t * UNROLL + u],
                        preferred_element_type=F32,
                    )
                )
            for spot, term in zip(spots, terms):
                total[spot] += term
            return carry

        lax.fori_loop(0, slots // UNROLL, turn, 0)

    def each(act):
        for i, dz in enumerate(where):
            target = z + dz
            valid = jnp.logical_and(target >= 0, target < nz)
            safe = jnp.where(valid, target, 0)

            @pl.when(valid)
            def _():
                act(
                    pltpu.make_async_copy(
                        total.at[pl.ds((2 * safe + y) * per, per)], keeps[i], keep_sems.at[i]
                    ),
                    pltpu.make_async_copy(staged.at[pl.ds(safe * per, per)], sends[i], send_sems.at[i]),
                )

    def narrow(i, carry):
        source = (2 * (i // per) + 1 - y) * per + i % per
        staged[i] = total[source].astype(BF16)
        return carry

    lax.fori_loop(0, nz * per, narrow, 0)
    each(lambda keep, send: (keep.start(), send.start()))
    each(lambda keep, send: (keep.wait(), send.wait()))


def backward(grid, codes, values, near, far, per):
    slots = values[0].shape[0]
    nz = grid.nz
    where = [0] + [d for k in range(1, nz) for d in (k, -k)]
    shape = (per, HALF, BLOCK)
    outs = pl.pallas_call(
        functools.partial(backward_kernel, nz, where),
        out_shape=[jax.ShapeDtypeStruct(shape, F32)] * len(where) + [jax.ShapeDtypeStruct(shape, BF16)] * len(where),
        in_specs=[SMEM, SMEM] + [ANY] * 4,
        out_specs=[ANY] * (2 * len(where)),
        scratch_shapes=[
            pltpu.VMEM((2 * slots, BLOCK, BLOCK), BF16),
            pltpu.VMEM((2 * RB_DEV, HALF, BLOCK), BF16),
            pltpu.VMEM((2 * nz * per + 1, HALF, BLOCK), F32),
            pltpu.VMEM((nz * per, HALF, BLOCK), BF16),
            pltpu.SemaphoreType.DMA((2,)),
            pltpu.SemaphoreType.DMA((2 * RB_DEV,)),
            pltpu.SemaphoreType.DMA((len(where),)),
            pltpu.SemaphoreType.DMA((len(where),)),
        ],
        name="backward",
    )(*codes, *values, near, far)
    return dict(zip(where, outs[: len(where)])), dict(zip(where, outs[len(where) :]))


def scatter_chips(grid, keeps, sends):
    nz = grid.nz
    move = functools.partial(lax.ppermute, axis_name="sample")
    rising = falling = None
    for d in range(nz - 1, 0, -1):
        for sign in (1, -1):
            if sign == 1:
                inside = lambda z: z <= nz - 1 - d
                perm = grid.up(inside)
            else:
                inside = lambda z: z >= d
                perm = grid.down(inside)
            part = keeps[sign * d] + move(sends[sign * d], perm=grid.along_y(inside)).astype(F32)
            before = rising if sign == 1 else falling
            if before is not None:
                part = part + before.astype(F32)
            moved = move(part.astype(BF16), perm=perm)
            if sign == 1:
                rising = moved
            else:
                falling = moved
    mine = keeps[0] + move(sends[0], perm=grid.along_y(lambda z: True)).astype(F32)
    return (mine + rising.astype(F32) + falling.astype(F32)).astype(BF16)


def sum_gram(grid, gram):
    move = functools.partial(lax.ppermute, axis_name="sample")
    _, _, core = position()
    part = gram.shape[0] // 2
    mine = lax.dynamic_slice_in_dim(gram, core * part, part, 0)
    theirs = lax.dynamic_slice_in_dim(gram, (1 - core) * part, part, 0)
    total = mine + move(theirs, perm=grid.core)
    total = total + lax.ppermute(total, "gene", grid.swap)
    total = total + move(total, perm=grid.along_y(lambda z: True))
    step = 1
    while step < grid.nz:
        total = total + move(total, perm=[(s, s ^ (4 * step)) for s in range(grid.n)])
        step *= 2
    other = move(total, perm=grid.core)
    return jnp.where(core == 0, jnp.concatenate([total, other]), jnp.concatenate([other, total]))


def whole_rows(grid, keep, send):
    _, _, core = position()
    part = (keep + lax.ppermute(send, "gene", grid.swap)).reshape(2, -1, HALF)
    other = lax.ppermute(part[1], "sample", grid.core)
    return jnp.where(
        core == 0,
        jnp.concatenate([part[0], other], axis=1),
        jnp.concatenate([other, part[0]], axis=1),
    )


def chip_local(grid, block_values, block_coords, block_counts, random_cols):
    _, _, core = position()
    move = functools.partial(lax.ppermute, axis_name="sample")
    slot_count = block_values.shape[0]
    cells = RB_DEV * BLOCK * grid.n
    used = jnp.arange(slot_count, dtype=jnp.int32) < block_counts[0]
    code = jnp.where(used, block_coords[:, 0], RB_DEV) * 65536 + block_coords[:, 1]
    codes = (code, move(code, perm=grid.core))
    values = (block_values, move(block_values, perm=grid.core))

    mine = lax.dynamic_slice_in_dim(random_cols, core * HALF, HALF, 1)
    theirs = lax.dynamic_slice_in_dim(random_cols, (1 - core) * HALF, HALF, 1)
    right = jnp.concatenate([mine, move(theirs, perm=grid.core)]).reshape(-1, BLOCK, HALF)
    per = right.shape[0]
    found = gather_chips(grid, right)
    sketch = whole_rows(grid, *forward(grid, codes, values, found, True, False))
    _, inverse = factor(sum_gram(grid, gram_of(sketch)), cells)
    first = lax.dot_general(
        inverse, sketch, (((1,), (1,)), ((), ())), precision=lax.Precision.HIGHEST, preferred_element_type=F32
    ).astype(BF16)
    mine = lax.dynamic_slice_in_dim(first, core * HALF, HALF, 0)
    theirs = lax.dynamic_slice_in_dim(first, (1 - core) * HALF, HALF, 0)
    near = jnp.stack([mine, move(theirs, perm=grid.core)])
    far = lax.ppermute(near, "gene", grid.swap)
    loadings = scatter_chips(grid, *backward(grid, codes, values, near, far, per))
    found = gather_chips(grid, loadings)
    second = whole_rows(grid, *forward(grid, codes, values, found, False, True))
    upper, inverse = factor(sum_gram(grid, gram_of(second)), cells)
    basis = lax.dot_general(
        second, inverse, (((1,), (1,)), ((), ())), precision=lax.Precision.HIGHEST, preferred_element_type=F32
    )
    return basis, upper


def take_forward(block_values, block_coords, alive, right_full):
    right_blocks = right_full.reshape(-1, BLOCK, RANK)
    picked = jnp.take(right_blocks, block_coords[:, 1], axis=0)
    products = jnp.einsum("nij,njk->nik", block_values, picked, preferred_element_type=F32)
    summed = jnp.zeros((RB_DEV, BLOCK, RANK), F32).at[block_coords[:, 0]].add(products * alive)
    return summed.reshape(RB_DEV * BLOCK, RANK)


def take_backward(block_values, block_coords, alive, left_rows, span_blocks):
    picked = jnp.take(left_rows.reshape(RB_DEV, BLOCK, RANK), block_coords[:, 0], axis=0)
    products = jnp.einsum("nij,nik->njk", block_values, picked, preferred_element_type=F32)
    summed = jnp.zeros((span_blocks, BLOCK, RANK), F32).at[block_coords[:, 1]].add(products * alive)
    return summed.reshape(span_blocks * BLOCK, RANK)


def any_local(n_sample, block_values, block_coords, block_counts, random_cols):
    cells = RB_DEV * BLOCK * n_sample
    alive = (jnp.arange(block_values.shape[0], dtype=jnp.int32) < block_counts[0]).astype(F32)[:, None, None]

    def basis_of(partial):
        summed = lax.psum_scatter(partial, "gene", scatter_dimension=0, tiled=True)
        upper, inverse = factor(lax.psum(gram_of(summed), ("sample", "gene")), cells)
        return jnp.dot(summed, inverse.T, precision=lax.Precision.HIGHEST, preferred_element_type=F32), upper

    random_full = lax.all_gather(random_cols, "sample", axis=0, tiled=True)
    first, _ = basis_of(take_forward(block_values, block_coords, alive, random_full))
    whole = lax.all_gather(first.astype(BF16), "gene", axis=0, tiled=True)
    part = take_backward(block_values, block_coords, alive, whole, random_full.shape[0] // BLOCK)
    mine = lax.psum_scatter(part, "sample", scatter_dimension=0, tiled=True).astype(BF16)
    loadings = lax.all_gather(mine, "sample", axis=0, tiled=True)
    return basis_of(take_forward(block_values, block_coords, alive, loadings))


def cores_are_samples(mesh):
    n_sample, n_gene = mesh.devices.shape
    if n_gene != 2 or n_sample % 4:
        return False
    chip = [tuple(d.coords) for d in mesh.devices[:, 0]]
    return all(chip[s] == chip[s ^ 1] for s in range(n_sample))


def solution(mesh):
    n_sample = mesh.shape["sample"]
    if cores_are_samples(mesh):
        body = functools.partial(chip_local, Grid(n_sample))
    else:
        body = functools.partial(any_local, n_sample)
    return jax.shard_map(
        body,
        mesh=mesh,
        in_specs=(
            P(("sample", "gene"), None, None),
            P(("sample", "gene"), None),
            P(("sample", "gene")),
            P(("gene", "sample"), None),
        ),
        out_specs=(P(("sample", "gene"), None), P()),
        check_vma=False,
    )
```

time: 920 us -> 341 us (0.37)
  waiting for transfers between devices: 584 us -> 158 us
  other arithmetic: 168 us -> 6.62 us
  starting transfers between devices: 0.75 us -> 108 us
  local copies, waits for them, and re-layouts: 84.3 us -> 5.16 us
  Pallas kernels: 0 us -> 54.1 us
  matrix products: 43.6 us -> 5.96 us
  between operations: 18.1 us -> 2.38 us
  loops' own time: 12.4 us -> 0 us
    psum x4 -> x0, waiting for transfers between devices: 256 us -> none  [the longest x2 178 us: orthonormal(): gram = lax.psum(gram_of(summed), 'sample')]
    reduce_scatter x1 -> x0, waiting for transfers between devices: 178 us -> none  [local(): lax.psum_scatter(loading_part, 'sample', scatter_dimension=0, tiled=True)]
    ppermute x0 -> x60, waiting for transfers between devices: none -> 158 us  [the longest x6 34.4 us: gather_chips(): falling = move(falling, perm=grid.down(lambda z: z <= nz - d))]
    all_gather x2 -> x0, waiting for transfers between devices: 149 us -> none  [the longest x1 75.6 us: local(): random_full = lax.all_gather(random_cols, 'sample', axis=0, tiled=True)]
    another operation x18 -> x1, other arithmetic: 112 us -> 0.03 us  [chip_local(): near = jnp.stack([mine, move(theirs, perm=grid.core)])]
    ppermute x0 -> x60, starting transfers between devices: none -> 108 us  [the longest x4 20.6 us: sum_gram(): total = total + move(total, perm=[(s, s ^ 4 * step) for s in range(grid.n)])]
    pallas_call x0 -> x5, Pallas kernels: none -> 54.1 us  [the longest x2 23.8 us: factor(): pl.pallas_call(functools.partial(factor_kernel, 1.0 / cells), out_shape=[...]
    scatter-add x6 -> x0, other arithmetic: 46 us -> none  [the longest x4 25.8 us: forward_product(): summed = summed.at[block_coords[offset:finish, 0]].add(weighted)]
  transfers between devices with their start and end apart: 7 -> 60, of which waited for: 7 -> 39; matrix products, arithmetic and copies ran while one was open for 0% -> 1% of each run, Pallas kernels for 0% -> 0%
where the time goes in v1:
time: 341 us; the launch traced here: 340 us
  waiting for transfers between devices  158 us (46%)
  starting transfers between devices  108 us (32%)
  Pallas kernels  54.1 us (16%)
  other arithmetic  6.62 us (2%)
  matrix products  5.96 us (2%)
  local copies, waits for them, and re-layouts  5.16 us (2%)
    ppermute x6, waiting for transfers between devices, gather_chips(): falling = move(falling, perm=grid.down(lambda z: z <= nz - d))  34.4 us
    ppermute x6, waiting for transfers between devices, gather_chips(): move(falling, perm=grid.along_y(lambda z: z <= nz - 1 - d))  30.1 us
    pallas_call x2, Pallas kernels, factor(): pl.pallas_call(functools.partial(factor_kernel, 1.0 / cells), out_shape=[...  23.8 us
    ppermute x4, starting transfers between devices, sum_gram(): total = total + move(total, perm=[(s, s ^ 4 * step) for s in range(grid.n)])  20.6 us
    ppermute x6, starting transfers between devices, gather_chips(): move(falling, perm=grid.along_y(lambda z: z <= nz - 1 - d))  19.6 us
    pallas_call x2, Pallas kernels, forward(): pl.pallas_call(functools.partial(forward_kernel, grid.nz, [spot[:2] for s...  19.3 us
    ppermute x2, waiting for transfers between devices, whole_rows(): part = (keep + lax.ppermute(send, 'gene', grid.swap)).reshape(2, -1, HALF)  18.9 us
    ppermute x6, waiting for transfers between devices, scatter_chips(): move(sends[sign * d], perm=grid.along_y(inside)).astype(F32)  17.4 us
  transfers between devices with their start and end apart: 60, of which 39 were waited for; matrix products, arithmetic and copies ran while one was open for 1% of the time, Pallas kernels for 0%

profile of v1, /device:TPU:0, one launch (start us, length us, event | category | flops | bytes accessed | tf_op | source)
XLA Modules:
  0.0 340.2 jit_solution(10516675479709613729)
XLA Ops:
  5.0 5.5 %collective-permute-start.4 = (bf16[16,128,128]{2,1,0:T(8,128)(2,1)S(1)}, bf16[16,128,128]{2,1,0:T(8,128)(2,1)S(1)}, u32[]{:S(2)}, u32[]{:S(2)}) collective-permute-start(bf16[16,128,128]{2,1,0:T(8,128)(2,1)S(1)} %bitcast.17), channel_id=1, source_target_pairs={{0,8},{2,10},{4,12},{6,14},{8,16},{10,18},{12,20},{14,22},{16,24},... | collective-permute-start | bytes 1572872 | tf_op jit(solution)/shard_map/ppermute | solution.py:110
  10.6 2.0 collective-permute-start.3
  12.6 8.1 %collective-permute-done.5.refs_3_ = bf16[16,128,128]{2,1,0:T(8,128)(2,1)S(1)} collective-permute-done((bf16[16,128,128]{2,1,0:T(8,128)(2,1)S(1)}, bf16[16,128,128]{2,1,0:T(8,128)(2,1)S(1)}, u32[]{:S(2)}, u32[]{:S(2)}) %collective-permute-start.5) | collective-permute-done | bytes 524320 | tf_op jit(solution)/shard_map/ppermute | solution.py:111
  24.6 3.6 %collective-permute-start.7 = (bf16[16,128,128]{2,1,0:T(8,128)(2,1)S(1)}, bf16[16,128,128]{2,1,0:T(8,128)(2,1)S(1)}, u32[]{:S(2)}, u32[]{:S(2)}) collective-permute-start(bf16[16,128,128]{2,1,0:T(8,128)(2,1)S(1)} %collective-permute-done.5.refs_3_), channel_id=1, source_target_pairs={{0,4},{2,6},{4,0},{6,2},{8,12},{10,14},{12,8},{14,10},{16,20},{18,... | collective-permute-start | bytes 1572872 | tf_op jit(solution)/shard_map/ppermute | solution.py:115
  28.9 7.0 %collective-permute-done.9.refs_7_ = bf16[16,128,128]{2,1,0:T(8,128)(2,1)S(1)} collective-permute-done((bf16[16,128,128]{2,1,0:T(8,128)(2,1)S(1)}, bf16[16,128,128]{2,1,0:T(8,128)(2,1)S(1)}, u32[]{:S(2)}, u32[]{:S(2)}) %collective-permute-start.9) | collective-permute-done | bytes 524320 | tf_op jit(solution)/shard_map/ppermute | solution.py:111
  38.0 2.5 collective-permute-done.7.refs_5_
  40.5 3.6 %collective-permute-start.11 = (bf16[16,128,128]{2,1,0:T(8,128)(2,1)S(1)}, bf16[16,128,128]{2,1,0:T(8,128)(2,1)S(1)}, u32[]{:S(2)}, u32[]{:S(2)}) collective-permute-start(bf16[16,128,128]{2,1,0:T(8,128)(2,1)S(1)} %collective-permute-done.9.refs_7_), channel_id=1, source_target_pairs={{0,4},{2,6},{4,0},{6,2},{8,12},{10,14},{12,8},{14,10},{1,5},{3,7},... | collective-permute-start | bytes 1572872 | tf_op jit(solution)/shard_map/ppermute | solution.py:115
  44.8 5.6 %collective-permute-done.13.refs_11_ = bf16[16,128,128]{2,1,0:T(8,128)(2,1)S(1)} collective-permute-done((bf16[16,128,128]{2,1,0:T(8,128)(2,1)S(1)}, bf16[16,128,128]{2,1,0:T(8,128)(2,1)S(1)}, u32[]{:S(2)}, u32[]{:S(2)}) %collective-permute-start.13) | collective-permute-done | bytes 524320 | tf_op jit(solution)/shard_map/ppermute | solution.py:111
  50.4 3.0 collective-permute-start.15
  53.5 1.5 collective-permute-start.14
  54.9 2.3 collective-permute-done.11.refs_9_
  58.6 8.2 %collective-permute-done.15.refs_13_ = bf16[16,128,128]{2,1,0:T(8,128)(2,1)S(1)} collective-permute-done((bf16[16,128,128]{2,1,0:T(8,128)(2,1)S(1)}, bf16[16,128,128]{2,1,0:T(8,128)(2,1)S(1)}, u32[]{:S(2)}, u32[]{:S(2)}) %collective-permute-start.15) | collective-permute-done | bytes 524320 | tf_op jit(solution)/shard_map/ppermute | solution.py:115
  67.7 9.0 %forward.2 = (f32[2,4,128,128]{3,2,1,0:T(8,128)}, f32[2,4,128,128]{3,2,1,0:T(8,128)}) custom-call(s32[64]{0:T(128)} %copy-done.36, s32[64]{0:T(128)} %copy-done.37, bf16[64,128,128]{2,1,0:T(8,128)(2,1)} %own_hbm.5, bf16[64,128,128]{2,1,0:T(8,128)(2,1)} %copy-done.1, bf16[16,128,128]{2,1,0:T(8,128)(2,1)} %bitcast.19, bf16[16,128,128]{2,1,0:T(8,128)(2,1)} %copy-done.13, ...), custom_call_target="tpu_custom_call" | custom-call | tf_op jit(solution)/shard_map/forward/pallas_call | solution.py:204
  76.7 1.7 collective-permute-start.16
  78.4 10.8 %collective-permute-done.16 = f32[2,4,128,128]{3,2,1,0:T(8,128)S(1)} collective-permute-done((f32[2,4,128,128]{3,2,1,0:T(8,128)}, f32[2,4,128,128]{3,2,1,0:T(8,128)S(1)}, u32[]{:S(2)}, u32[]{:S(2)}) %collective-permute-start.16) | collective-permute-done | bytes 524320 | tf_op jit(solution)/shard_map/ppermute | solution.py:366
  90.5 1.5 collective-permute-done.17
  94.5 1.7 collective-permute-start.19
  96.2 3.9 %collective-permute-done.19 = f32[128,256]{1,0:T(8,128)S(1)} collective-permute-done((f32[128,256]{1,0:T(8,128)S(1)}, f32[128,256]{1,0:T(8,128)S(1)}, u32[]{:S(2)}, u32[]{:S(2)}) %collective-permute-start.19) | collective-permute-done | bytes 131104 | tf_op jit(solution)/shard_map/ppermute | solution.py:354
  100.1 1.7 collective-permute-start.20
  101.9 3.3 collective-permute-done.20
  105.2 4.4 %collective-permute-start.21 = (f32[128,256]{1,0:T(8,128)S(1)}, f32[128,256]{1,0:T(8,128)S(1)}, u32[]{:S(2)}, u32[]{:S(2)}) collective-permute-start(f32[128,256]{1,0:T(8,128)S(1)} %add.105), channel_id=1, source_target_pairs={{0,8},{2,10},{4,12},{6,14},{8,0},{10,2},{12,4},{14,6},{16,24},{18,... | collective-permute-start | bytes 393224 | tf_op jit(solution)/shard_map/ppermute | solution.py:358
  109.6 2.9 collective-permute-done.21
  112.5 6.5 %collective-permute-start.22 = (f32[128,256]{1,0:T(8,128)S(1)}, f32[128,256]{1,0:T(8,128)S(1)}, u32[]{:S(2)}, u32[]{:S(2)}) collective-permute-start(f32[128,256]{1,0:T(8,128)S(1)} %add.106), channel_id=1, source_target_pairs={{0,16},{2,18},{4,20},{6,22},{8,24},{10,26},{12,28},{14,30},{16,0},... | collective-permute-start | bytes 393224 | tf_op jit(solution)/shard_map/ppermute | solution.py:358
  119.1 3.3 collective-permute-done.22
  124.6 11.9 %factor.2 = (f32[256,256]{1,0:T(8,128)}, f32[256,256]{1,0:T(8,128)}) custom-call(f32[256,256]{1,0:T(8,128)} %maximum_select_fusion.6.gram_ref), custom_call_target="tpu_custom_call" | custom-call | tf_op jit(solution)/shard_map/factor/pallas_call | solution.py:71
  136.5 1.6 convolution_convert_fusion
  139.6 1.5 collective-permute-start.25
  141.1 6.9 %collective-permute-done.25.far_hbm = bf16[2,128,512]{2,1,0:T(8,128)(2,1)S(1)} collective-permute-done((bf16[2,128,512]{2,1,0:T(8,128)(2,1)S(1)}, bf16[2,128,512]{2,1,0:T(8,128)(2,1)S(1)}, u32[]{:S(2)}, u32[]{:S(2)}) %collective-permute-start.25) | collective-permute-done | bytes 262176 | tf_op jit(solution)/shard_map/ppermute | solution.py:398
  148.7 10.9 %backward.1 = (f32[16,128,128]{2,1,0:T(8,128)}, f32[16,128,128]{2,1,0:T(8,128)}, f32[16,128,128]{2,1,0:T(8,128)}, f32[16,128,128]{2,1,0:T(8,128)}, f32[16,128,12...) custom-call(s32[64]{0:T(128)} %copy-done.36, ...), custom_call_target="tpu_custom_call" | custom-call | tf_op jit(solution)/shard_map/backward/pallas_call | solution.py:302
  159.6 3.5 %collective-permute-start.29 = (bf16[16,128,128]{2,1,0:T(8,128)(2,1)}, bf16[16,128,128]{2,1,0:T(8,128)(2,1)S(1)}, u32[]{:S(2)}, u32[]{:S(2)}) collective-permute-start(bf16[16,128,128]{2,1,0:T(8,128)(2,1)} %get-tuple-element.33), channel_id=1, source_target_pairs={{0,4},{2,6},{4,0},{6,2},{1,5},{3,7},{5,1},{7,3}} | collective-permute-start | bytes 1572872 | tf_op jit(solution)/shard_map/ppermute | solution.py:334
  163.8 2.4 collective-permute-start.28
  166.3 10.3 %collective-permute-done.29 = bf16[16,128,128]{2,1,0:T(8,128)(2,1)S(1)} collective-permute-done((bf16[16,128,128]{2,1,0:T(8,128)(2,1)}, bf16[16,128,128]{2,1,0:T(8,128)(2,1)S(1)}, u32[]{:S(2)}, u32[]{:S(2)}) %collective-permute-start.29) | collective-permute-done | bytes 524320 | tf_op jit(solution)/shard_map/ppermute | solution.py:334
  176.6 1.5 add_convert_fusion.6
  181.2 3.4 %collective-permute-start.27 = (bf16[16,128,128]{2,1,0:T(8,128)(2,1)S(1)}, bf16[16,128,128]{2,1,0:T(8,128)(2,1)S(1)}, u32[]{:S(2)}, u32[]{:S(2)}) collective-permute-start(bf16[16,128,128]{2,1,0:T(8,128)(2,1)S(1)} %copy-done.41), channel_id=1, source_target_pairs={{0,4},{2,6},{4,0},{6,2},{8,12},{10,14},{12,8},{14,10},{16,20},{18,... | collective-permute-start | bytes 1572872 | tf_op jit(solution)/shard_map/ppermute | solution.py:334
  184.6 3.2 collective-permute-done.28
  188.8 3.8 %collective-permute-start.31 = (bf16[16,128,128]{2,1,0:T(8,128)(2,1)S(1)}, bf16[16,128,128]{2,1,0:T(8,128)(2,1)S(1)}, u32[]{:S(2)}, u32[]{:S(2)}) collective-permute-start(bf16[16,128,128]{2,1,0:T(8,128)(2,1)S(1)} %add_convert_fusion.5), channel_id=1, source_target_pairs={{0,8},{2,10},{4,12},{6,14},{8,16},{10,18},{12,20},{14,22},{1,9},{3... | collective-permute-start | bytes 1572872 | tf_op jit(solution)/shard_map/ppermute | solution.py:338
  193.7 1.5 collective-permute-start.26
  195.2 3.9 %collective-permute-done.27 = bf16[16,128,128]{2,1,0:T(8,128)(2,1)S(1)} collective-permute-done((bf16[16,128,128]{2,1,0:T(8,128)(2,1)S(1)}, bf16[16,128,128]{2,1,0:T(8,128)(2,1)S(1)}, u32[]{:S(2)}, u32[]{:S(2)}) %collective-permute-start.27) | collective-permute-done | bytes 524320 | tf_op jit(solution)/shard_map/ppermute | solution.py:334
  200.4 4.5 %collective-permute-start.32 = (bf16[16,128,128]{2,1,0:T(8,128)(2,1)S(1)}, bf16[16,128,128]{2,1,0:T(8,128)(2,1)S(1)}, u32[]{:S(2)}, u32[]{:S(2)}) collective-permute-start(bf16[16,128,128]{2,1,0:T(8,128)(2,1)S(1)} %add_convert_fusion.4), channel_id=1, source_target_pairs={{0,8},{2,10},{4,12},{6,14},{8,16},{10,18},{12,20},{14,22},{16,24},... | collective-permute-start | bytes 1572872 | tf_op jit(solution)/shard_map/ppermute | solution.py:338
  206.4 2.2 collective-permute-done.26
  208.7 2.9 collective-permute-done.32
  211.6 5.2 %collective-permute-done.38 = bf16[16,128,128]{2,1,0:T(8,128)(2,1)S(1)} collective-permute-done((bf16[16,128,128]{2,1,0:T(8,128)(2,1)S(1)}, bf16[16,128,128]{2,1,0:T(8,128)(2,1)S(1)}, u32[]{:S(2)}, u32[]{:S(2)}) %collective-permute-start.38) | collective-permute-done | bytes 524320 | tf_op jit(solution)/shard_map/ppermute | solution.py:338
  218.3 4.6 %collective-permute-start.40 = (bf16[16,128,128]{2,1,0:T(8,128)(2,1)S(1)}, bf16[16,128,128]{2,1,0:T(8,128)(2,1)S(1)}, u32[]{:S(2)}, u32[]{:S(2)}) collective-permute-start(bf16[16,128,128]{2,1,0:T(8,128)(2,1)S(1)} %add_convert_fusion.refs_0_), channel_id=1, source_target_pairs={{0,8},{2,10},{4,12},{6,14},{8,16},{10,18},{12,20},{14,22},{16,24},... | collective-permute-start | bytes 1572872 | tf_op jit(solution)/shard_map/ppermute | solution.py:110
  222.9 6.3 %collective-permute-done.41.refs_3_ = bf16[16,128,128]{2,1,0:T(8,128)(2,1)S(1)} collective-permute-done((bf16[16,128,128]{2,1,0:T(8,128)(2,1)S(1)}, bf16[16,128,128]{2,1,0:T(8,128)(2,1)S(1)}, u32[]{:S(2)}, u32[]{:S(2)}) %collective-permute-start.41) | collective-permute-done | bytes 524320 | tf_op jit(solution)/shard_map/ppermute | solution.py:111
  232.0 3.2 collective-permute-start.43
  235.2 7.3 %collective-permute-done.45.refs_7_ = bf16[16,128,128]{2,1,0:T(8,128)(2,1)S(1)} collective-permute-done((bf16[16,128,128]{2,1,0:T(8,128)(2,1)S(1)}, bf16[16,128,128]{2,1,0:T(8,128)(2,1)S(1)}, u32[]{:S(2)}, u32[]{:S(2)}) %collective-permute-start.45) | collective-permute-done | bytes 524320 | tf_op jit(solution)/shard_map/ppermute | solution.py:111
  245.6 3.1 collective-permute-start.47
  248.7 8.1 %collective-permute-done.43.refs_5_ = bf16[16,128,128]{2,1,0:T(8,128)(2,1)S(1)} collective-permute-done((bf16[16,128,128]{2,1,0:T(8,128)(2,1)S(1)}, bf16[16,128,128]{2,1,0:T(8,128)(2,1)S(1)}, u32[]{:S(2)}, u32[]{:S(2)}) %collective-permute-start.43) | collective-permute-done | bytes 524320 | tf_op jit(solution)/shard_map/ppermute | solution.py:115
  257.5 3.2 collective-permute-start.51
  260.7 1.5 collective-permute-start.50
  262.2 3.5 %collective-permute-done.47.refs_9_ = bf16[16,128,128]{2,1,0:T(8,128)(2,1)S(1)} collective-permute-done((bf16[16,128,128]{2,1,0:T(8,128)(2,1)S(1)}, bf16[16,128,128]{2,1,0:T(8,128)(2,1)S(1)}, u32[]{:S(2)}, u32[]{:S(2)}) %collective-permute-start.47) | collective-permute-done | bytes 524320 | tf_op jit(solution)/shard_map/ppermute | solution.py:115
  265.7 5.6 %collective-permute-done.51.refs_13_ = bf16[16,128,128]{2,1,0:T(8,128)(2,1)S(1)} collective-permute-done((bf16[16,128,128]{2,1,0:T(8,128)(2,1)S(1)}, bf16[16,128,128]{2,1,0:T(8,128)(2,1)S(1)}, u32[]{:S(2)}, u32[]{:S(2)}) %collective-permute-start.51) | collective-permute-done | bytes 524320 | tf_op jit(solution)/shard_map/ppermute | solution.py:115
  272.2 10.3 %forward.3 = (f32[2,4,128,128]{3,2,1,0:T(8,128)}, f32[2,4,128,128]{3,2,1,0:T(8,128)}) custom-call(s32[64]{0:T(128)} %copy-done.36, s32[64]{0:T(128)} %copy-done.37, bf16[64,128,128]{2,1,0:T(8,128)(2,1)} %own_hbm.5, bf16[64,128,128]{2,1,0:T(8,128)(2,1)} %copy-done.1, bf16[16,128,128]{2,1,0:T(8,128)(2,1)} %copy-done.3, bf16[16,128,128]{2,1,0:T(8,128)(2,1)} %copy-done.20, ...), custom_call_target="tpu_custom_call" | custom-call | tf_op jit(solution)/shard_map/forward/pallas_call | solution.py:204
  283.9 8.0 %collective-permute-done.52 = f32[2,4,128,128]{3,2,1,0:T(8,128)S(1)} collective-permute-done((f32[2,4,128,128]{3,2,1,0:T(8,128)}, f32[2,4,128,128]{3,2,1,0:T(8,128)S(1)}, u32[]{:S(2)}, u32[]{:S(2)}) %collective-permute-start.52) | collective-permute-done | bytes 524320 | tf_op jit(solution)/shard_map/ppermute | solution.py:366
  293.2 1.5 collective-permute-done.53
  298.6 4.2 %collective-permute-done.55 = f32[128,256]{1,0:T(8,128)S(1)} collective-permute-done((f32[128,256]{1,0:T(8,128)S(1)}, f32[128,256]{1,0:T(8,128)S(1)}, u32[]{:S(2)}, u32[]{:S(2)}) %collective-permute-start.55) | collective-permute-done | bytes 131104 | tf_op jit(solution)/shard_map/ppermute | solution.py:354
  302.8 1.4 collective-permute-start.56
  304.3 3.6 %collective-permute-done.56 = f32[128,256]{1,0:T(8,128)S(1)} collective-permute-done((f32[128,256]{1,0:T(8,128)S(1)}, f32[128,256]{1,0:T(8,128)S(1)}, u32[]{:S(2)}, u32[]{:S(2)}) %collective-permute-start.56) | collective-permute-done | bytes 131104 | tf_op jit(solution)/shard_map/ppermute | solution.py:355
  307.9 7.0 %collective-permute-start.57 = (f32[128,256]{1,0:T(8,128)S(1)}, f32[128,256]{1,0:T(8,128)S(1)}, u32[]{:S(2)}, u32[]{:S(2)}) collective-permute-start(f32[128,256]{1,0:T(8,128)S(1)} %add.124), channel_id=1, source_target_pairs={{0,8},{2,10},{4,12},{6,14},{8,0},{10,2},{12,4},{14,6},{16,24},{18,... | collective-permute-start | bytes 393224 | tf_op jit(solution)/shard_map/ppermute | solution.py:358
  314.9 2.9 collective-permute-done.57
  317.8 2.7 collective-permute-start.58
  320.6 3.2 collective-permute-done.58
  325.9 11.9 %factor.3 = (f32[256,256]{1,0:T(8,128)}, f32[256,256]{1,0:T(8,128)}) custom-call(f32[256,256]{1,0:T(8,128)} %maximum_select_fusion.7.gram_ref), custom_call_target="tpu_custom_call" | custom-call | tf_op jit(solution)/shard_map/factor/pallas_call | solution.py:71
  337.9 2.4 fusion
  (181 shorter events, 47.2 us)
Async XLA Ops:
  1.9 1.7 collective-permute-start.2
  3.6 64.0 %copy-start.2 = (bf16[2048,128]{1,0:T(8,128)(2,1)}, bf16[2048,128]{1,0:T(8,128)(2,1)S(1)}, u32[]{:S(2)}) copy-start(bf16[2048,128]{1,0:T(8,128)(2,1)S(1)} %pad_maximum_fusion) | copy-start | bytes 1572868
  3.7 17.1 %collective-permute-start.5 = (bf16[16,128,128]{2,1,0:T(8,128)(2,1)S(1)}, bf16[16,128,128]{2,1,0:T(8,128)(2,1)S(1)}, u32[]{:S(2)}, u32[]{:S(2)}) collective-permute-start(bf16[16,128,128]{2,1,0:T(8,128)(2,1)S(1)} %bitcast.16), channel_id=1, source_target_pairs={{8,0},{10,2},{12,4},{14,6},{16,8},{18,10},{20,12},{22,14},{24,16},... | collective-permute-start | bytes 1572872 | tf_op jit(solution)/shard_map/ppermute | solution.py:111
  5.0 17.1 %collective-permute-start.4 = (bf16[16,128,128]{2,1,0:T(8,128)(2,1)S(1)}, bf16[16,128,128]{2,1,0:T(8,128)(2,1)S(1)}, u32[]{:S(2)}, u32[]{:S(2)}) collective-permute-start(bf16[16,128,128]{2,1,0:T(8,128)(2,1)S(1)} %bitcast.17), channel_id=1, source_target_pairs={{0,8},{2,10},{4,12},{6,14},{8,16},{10,18},{12,20},{14,22},{16,24},... | collective-permute-start | bytes 1572872 | tf_op jit(solution)/shard_map/ppermute | solution.py:110
  10.5 46.7 %collective-permute-start.1 = (bf16[64,128,128]{2,1,0:T(8,128)(2,1)S(1)}, bf16[64,128,128]{2,1,0:T(8,128)(2,1)S(1)}, u32[]{:S(2)}, u32[]{:S(2)}) collective-permute-start(bf16[64,128,128]{2,1,0:T(8,128)(2,1)S(1)} %copy-done), channel_id=1, source_target_pairs={{0,2},{2,0},{4,6},{6,4},{8,10},{10,8},{12,14},{14,12},{16,18},{18,... | collective-permute-start | bytes 6291464 | tf_op jit(solution)/shard_map/ppermute | solution.py:383
  10.6 17.7 %collective-permute-start.3 = (bf16[16,128,128]{2,1,0:T(8,128)(2,1)S(1)}, bf16[16,128,128]{2,1,0:T(8,128)(2,1)S(1)}, u32[]{:S(2)}, u32[]{:S(2)}) collective-permute-start(bf16[16,128,128]{2,1,0:T(8,128)(2,1)S(1)} %bitcast.18), channel_id=1, source_target_pairs={{0,4},{2,6},{4,0},{6,2},{8,12},{10,14},{12,8},{14,10},{16,20},{18,... | collective-permute-start | bytes 1572872 | tf_op jit(solution)/shard_map/ppermute | solution.py:107
  20.7 47.0 %copy-start.11 = (bf16[16,128,128]{2,1,0:T(8,128)(2,1)}, bf16[16,128,128]{2,1,0:T(8,128)(2,1)S(1)}, u32[]{:S(2)}) copy-start(bf16[16,128,128]{2,1,0:T(8,128)(2,1)S(1)} %collective-permute-done.5.refs_3_) | copy-start | bytes 1572868
  20.7 15.3 %collective-permute-start.9 = (bf16[16,128,128]{2,1,0:T(8,128)(2,1)S(1)}, bf16[16,128,128]{2,1,0:T(8,128)(2,1)S(1)}, u32[]{:S(2)}, u32[]{:S(2)}) collective-permute-start(bf16[16,128,128]{2,1,0:T(8,128)(2,1)S(1)} %collective-permute-done.5.refs_3_), channel_id=1, source_target_pairs={{8,0},{10,2},{12,4},{14,6},{16,8},{18,10},{20,12},{22,14},{9,1},{1... | collective-permute-start | bytes 1572872 | tf_op jit(solution)/shard_map/ppermute | solution.py:111
  22.0 44.8 %copy-start.12 = (bf16[16,128,128]{2,1,0:T(8,128)(2,1)}, bf16[16,128,128]{2,1,0:T(8,128)(2,1)S(1)}, u32[]{:S(2)}) copy-start(bf16[16,128,128]{2,1,0:T(8,128)(2,1)S(1)} %collective-permute-done.4.refs_2_) | copy-start | bytes 1572868
  22.0 15.3 %collective-permute-start.8 = (bf16[16,128,128]{2,1,0:T(8,128)(2,1)S(1)}, bf16[16,128,128]{2,1,0:T(8,128)(2,1)S(1)}, u32[]{:S(2)}, u32[]{:S(2)}) collective-permute-start(bf16[16,128,128]{2,1,0:T(8,128)(2,1)S(1)} %collective-permute-done.4.refs_2_), channel_id=1, source_target_pairs={{8,16},{10,18},{12,20},{14,22},{16,24},{18,26},{20,28},{22,30},{9,... | collective-permute-start | bytes 1572872 | tf_op jit(solution)/shard_map/ppermute | solution.py:110
  23.4 1.2 collective-permute-start
  24.6 15.9 %collective-permute-start.7 = (bf16[16,128,128]{2,1,0:T(8,128)(2,1)S(1)}, bf16[16,128,128]{2,1,0:T(8,128)(2,1)S(1)}, u32[]{:S(2)}, u32[]{:S(2)}) collective-permute-start(bf16[16,128,128]{2,1,0:T(8,128)(2,1)S(1)} %collective-permute-done.5.refs_3_), channel_id=1, source_target_pairs={{0,4},{2,6},{4,0},{6,2},{8,12},{10,14},{12,8},{14,10},{16,20},{18,... | collective-permute-start | bytes 1572872 | tf_op jit(solution)/shard_map/ppermute | solution.py:115
  28.2 15.9 %collective-permute-start.6 = (bf16[16,128,128]{2,1,0:T(8,128)(2,1)S(1)}, bf16[16,128,128]{2,1,0:T(8,128)(2,1)S(1)}, u32[]{:S(2)}, u32[]{:S(2)}) collective-permute-start(bf16[16,128,128]{2,1,0:T(8,128)(2,1)S(1)} %collective-permute-done.4.refs_2_), channel_id=1, source_target_pairs={{8,12},{10,14},{12,8},{14,10},{16,20},{18,22},{20,16},{22,18},{24,... | collective-permute-start | bytes 1572872 | tf_op jit(solution)/shard_map/ppermute | solution.py:114
  36.0 14.4 %collective-permute-start.13 = (bf16[16,128,128]{2,1,0:T(8,128)(2,1)S(1)}, bf16[16,128,128]{2,1,0:T(8,128)(2,1)S(1)}, u32[]{:S(2)}, u32[]{:S(2)}) collective-permute-start(bf16[16,128,128]{2,1,0:T(8,128)(2,1)S(1)} %collective-permute-done.9.refs_7_), channel_id=1, source_target_pairs={{8,0},{10,2},{12,4},{14,6},{9,1},{11,3},{13,5},{15,7}} | collective-permute-start | bytes 1572872 | tf_op jit(solution)/shard_map/ppermute | solution.py:111
  37.3 16.1 %collective-permute-start.12 = (bf16[16,128,128]{2,1,0:T(8,128)(2,1)S(1)}, bf16[16,128,128]{2,1,0:T(8,128)(2,1)S(1)}, u32[]{:S(2)}, u32[]{:S(2)}) collective-permute-start(bf16[16,128,128]{2,1,0:T(8,128)(2,1)S(1)} %collective-permute-done.8.refs_6_), channel_id=1, source_target_pairs={{16,24},{18,26},{20,28},{22,30},{17,25},{19,27},{21,29},{23,31}} | collective-permute-start | bytes 1572872 | tf_op jit(solution)/shard_map/ppermute | solution.py:110
  40.5 16.7 %collective-permute-start.11 = (bf16[16,128,128]{2,1,0:T(8,128)(2,1)S(1)}, bf16[16,128,128]{2,1,0:T(8,128)(2,1)S(1)}, u32[]{:S(2)}, u32[]{:S(2)}) collective-permute-start(bf16[16,128,128]{2,1,0:T(8,128)(2,1)S(1)} %collective-permute-done.9.refs_7_), channel_id=1, source_target_pairs={{0,4},{2,6},{4,0},{6,2},{8,12},{10,14},{12,8},{14,10},{1,5},{3,7},... | collective-permute-start | bytes 1572872 | tf_op jit(solution)/shard_map/ppermute | solution.py:115
  44.1 13.1 %collective-permute-start.10 = (bf16[16,128,128]{2,1,0:T(8,128)(2,1)S(1)}, bf16[16,128,128]{2,1,0:T(8,128)(2,1)S(1)}, u32[]{:S(2)}, u32[]{:S(2)}) collective-permute-start(bf16[16,128,128]{2,1,0:T(8,128)(2,1)S(1)} %collective-permute-done.8.refs_6_), channel_id=1, source_target_pairs={{16,20},{18,22},{20,16},{22,18},{24,28},{26,30},{28,24},{30,26},{1... | collective-permute-start | bytes 1572872 | tf_op jit(solution)/shard_map/ppermute | solution.py:114
  50.4 16.4 %collective-permute-start.15 = (bf16[16,128,128]{2,1,0:T(8,128)(2,1)S(1)}, bf16[16,128,128]{2,1,0:T(8,128)(2,1)S(1)}, u32[]{:S(2)}, u32[]{:S(2)}) collective-permute-start(bf16[16,128,128]{2,1,0:T(8,128)(2,1)S(1)} %collective-permute-done.13.refs_11_), channel_id=1, source_target_pairs={{0,4},{2,6},{4,0},{6,2},{1,5},{3,7},{5,1},{7,3}} | collective-permute-start | bytes 1572872 | tf_op jit(solution)/shard_map/ppermute | solution.py:115
  53.5 14.2 %collective-permute-start.14 = (bf16[16,128,128]{2,1,0:T(8,128)(2,1)S(1)}, bf16[16,128,128]{2,1,0:T(8,128)(2,1)}, u32[]{:S(2)}, u32[]{:S(2)}) collective-permute-start(bf16[16,128,128]{2,1,0:T(8,128)(2,1)S(1)} %collective-permute-done.12.refs_10_), channel_id=1, source_target_pairs={{24,28},{26,30},{28,24},{30,26},{25,29},{27,31},{29,25},{31,27}} | collective-permute-start | bytes 1572872 | tf_op jit(solution)/shard_map/ppermute | solution.py:114
  76.7 12.5 %collective-permute-start.16 = (f32[2,4,128,128]{3,2,1,0:T(8,128)}, f32[2,4,128,128]{3,2,1,0:T(8,128)S(1)}, u32[]{:S(2)}, u32[]{:S(2)}) collective-permute-start(f32[2,4,128,128]{3,2,1,0:T(8,128)} %get-tuple-element.24), channel_id=1, source_target_pairs={{0,1},{1,0},{2,3},{3,2},{4,5},{5,4},{6,7},{7,6},{8,9},{9,8},{10,11... | collective-permute-start | bytes 1572872 | tf_op jit(solution)/shard_map/ppermute | solution.py:366
  90.4 1.6 collective-permute-start.17
  93.1 1.4 collective-permute-start.18
  94.5 5.6 %collective-permute-start.19 = (f32[128,256]{1,0:T(8,128)S(1)}, f32[128,256]{1,0:T(8,128)S(1)}, u32[]{:S(2)}, u32[]{:S(2)}) collective-permute-start(f32[128,256]{1,0:T(8,128)S(1)} %dynamic-slice_add_fusion.1), channel_id=1, source_target_pairs={{0,1},{1,0},{2,3},{3,2},{4,5},{5,4},{6,7},{7,6},{8,9},{9,8},{10,11... | collective-permute-start | bytes 393224 | tf_op jit(solution)/shard_map/ppermute | solution.py:354
  100.1 5.0 %collective-permute-start.20 = (f32[128,256]{1,0:T(8,128)S(1)}, f32[128,256]{1,0:T(8,128)S(1)}, u32[]{:S(2)}, u32[]{:S(2)}) collective-permute-start(f32[128,256]{1,0:T(8,128)S(1)} %add.104), channel_id=1, source_target_pairs={{0,4},{2,6},{4,0},{6,2},{8,12},{10,14},{12,8},{14,10},{16,20},{18,... | collective-permute-start | bytes 393224 | tf_op jit(solution)/shard_map/ppermute | solution.py:355
  105.2 7.3 %collective-permute-start.21 = (f32[128,256]{1,0:T(8,128)S(1)}, f32[128,256]{1,0:T(8,128)S(1)}, u32[]{:S(2)}, u32[]{:S(2)}) collective-permute-start(f32[128,256]{1,0:T(8,128)S(1)} %add.105), channel_id=1, source_target_pairs={{0,8},{2,10},{4,12},{6,14},{8,0},{10,2},{12,4},{14,6},{16,24},{18,... | collective-permute-start | bytes 393224 | tf_op jit(solution)/shard_map/ppermute | solution.py:358
  112.5 9.9 %collective-permute-start.22 = (f32[128,256]{1,0:T(8,128)S(1)}, f32[128,256]{1,0:T(8,128)S(1)}, u32[]{:S(2)}, u32[]{:S(2)}) collective-permute-start(f32[128,256]{1,0:T(8,128)S(1)} %add.106), channel_id=1, source_target_pairs={{0,16},{2,18},{4,20},{6,22},{8,24},{10,26},{12,28},{14,30},{16,0},... | collective-permute-start | bytes 393224 | tf_op jit(solution)/shard_map/ppermute | solution.py:358
  122.4 1.4 collective-permute-start.23
  138.1 1.4 collective-permute-start.24
  139.6 8.4 %collective-permute-start.25 = (bf16[2,128,512]{2,1,0:T(8,128)(2,1)S(1)}, bf16[2,128,512]{2,1,0:T(8,128)(2,1)S(1)}, u32[]{:S(2)}, u32[]{:S(2)}) collective-permute-start(bf16[2,128,512]{2,1,0:T(8,128)(2,1)S(1)} %pad_maximum_fusion.1.near_hbm), channel_id=1, source_target_pairs={{0,1},{1,0},{2,3},{3,2},{4,5},{5,4},{6,7},{7,6},{8,9},{9,8},{10,11... | collective-permute-start | bytes 786440 | tf_op jit(solution)/shard_map/ppermute | solution.py:398
  159.6 17.0 %collective-permute-start.29 = (bf16[16,128,128]{2,1,0:T(8,128)(2,1)}, bf16[16,128,128]{2,1,0:T(8,128)(2,1)S(1)}, u32[]{:S(2)}, u32[]{:S(2)}) collective-permute-start(bf16[16,128,128]{2,1,0:T(8,128)(2,1)} %get-tuple-element.33), channel_id=1, source_target_pairs={{0,4},{2,6},{4,0},{6,2},{1,5},{3,7},{5,1},{7,3}} | collective-permute-start | bytes 1572872 | tf_op jit(solution)/shard_map/ppermute | solution.py:334
  163.1 17.0 %collective-permute-start.35 = (bf16[16,128,128]{2,1,0:T(8,128)(2,1)}, bf16[16,128,128]{2,1,0:T(8,128)(2,1)S(1)}, u32[]{:S(2)}, u32[]{:S(2)}) collective-permute-start(bf16[16,128,128]{2,1,0:T(8,128)(2,1)} %get-tuple-element.39), channel_id=1, source_target_pairs={{24,28},{26,30},{28,24},{30,26},{25,29},{27,31},{29,25},{31,27}} | collective-permute-start | bytes 1572872 | tf_op jit(solution)/shard_map/ppermute | solution.py:334
  163.8 24.0 %collective-permute-start.28 = (bf16[16,128,128]{2,1,0:T(8,128)(2,1)}, bf16[16,128,128]{2,1,0:T(8,128)(2,1)S(1)}, u32[]{:S(2)}, u32[]{:S(2)}) collective-permute-start(bf16[16,128,128]{2,1,0:T(8,128)(2,1)} %get-tuple-element.31), channel_id=1, source_target_pairs={{0,4},{2,6},{4,0},{6,2},{8,12},{10,14},{12,8},{14,10},{1,5},{3,7},... | collective-permute-start | bytes 1572872 | tf_op jit(solution)/shard_map/ppermute | solution.py:334
  178.1 10.4 %collective-permute-start.30 = (bf16[16,128,128]{2,1,0:T(8,128)(2,1)S(1)}, bf16[16,128,128]{2,1,0:T(8,128)(2,1)S(1)}, u32[]{:S(2)}, u32[]{:S(2)}) collective-permute-start(bf16[16,128,128]{2,1,0:T(8,128)(2,1)S(1)} %add_convert_fusion.6), channel_id=1, source_target_pairs={{0,8},{2,10},{4,12},{6,14},{1,9},{3,11},{5,13},{7,15}} | collective-permute-start | bytes 1572872 | tf_op jit(solution)/shard_map/ppermute | solution.py:338
  179.5 13.1 %collective-permute-start.34 = (bf16[16,128,128]{2,1,0:T(8,128)(2,1)S(1)}, bf16[16,128,128]{2,1,0:T(8,128)(2,1)S(1)}, u32[]{:S(2)}, u32[]{:S(2)}) collective-permute-start(bf16[16,128,128]{2,1,0:T(8,128)(2,1)S(1)} %copy-done.42), channel_id=1, source_target_pairs={{16,20},{18,22},{20,16},{22,18},{24,28},{26,30},{28,24},{30,26},{1... | collective-permute-start | bytes 1572872 | tf_op jit(solution)/shard_map/ppermute | solution.py:334
  180.4 12.3 %collective-permute-start.36 = (bf16[16,128,128]{2,1,0:T(8,128)(2,1)S(1)}, bf16[16,128,128]{2,1,0:T(8,128)(2,1)S(1)}, u32[]{:S(2)}, u32[]{:S(2)}) collective-permute-start(bf16[16,128,128]{2,1,0:T(8,128)(2,1)S(1)} %add_convert_fusion.3), channel_id=1, source_target_pairs={{24,16},{26,18},{28,20},{30,22},{25,17},{27,19},{29,21},{31,23}} | collective-permute-start | bytes 1572872 | tf_op jit(solution)/shard_map/ppermute | solution.py:338
  181.2 17.9 %collective-permute-start.27 = (bf16[16,128,128]{2,1,0:T(8,128)(2,1)S(1)}, bf16[16,128,128]{2,1,0:T(8,128)(2,1)S(1)}, u32[]{:S(2)}, u32[]{:S(2)}) collective-permute-start(bf16[16,128,128]{2,1,0:T(8,128)(2,1)S(1)} %copy-done.41), channel_id=1, source_target_pairs={{0,4},{2,6},{4,0},{6,2},{8,12},{10,14},{12,8},{14,10},{16,20},{18,... | collective-permute-start | bytes 1572872 | tf_op jit(solution)/shard_map/ppermute | solution.py:334
  187.9 17.1 %collective-permute-start.33 = (bf16[16,128,128]{2,1,0:T(8,128)(2,1)S(1)}, bf16[16,128,128]{2,1,0:T(8,128)(2,1)S(1)}, u32[]{:S(2)}, u32[]{:S(2)}) collective-permute-start(bf16[16,128,128]{2,1,0:T(8,128)(2,1)S(1)} %copy-done.40), channel_id=1, source_target_pairs={{8,12},{10,14},{12,8},{14,10},{16,20},{18,22},{20,16},{22,18},{24,... | collective-permute-start | bytes 1572872 | tf_op jit(solution)/shard_map/ppermute | solution.py:334
  188.8 11.4 %collective-permute-start.31 = (bf16[16,128,128]{2,1,0:T(8,128)(2,1)S(1)}, bf16[16,128,128]{2,1,0:T(8,128)(2,1)S(1)}, u32[]{:S(2)}, u32[]{:S(2)}) collective-permute-start(bf16[16,128,128]{2,1,0:T(8,128)(2,1)S(1)} %add_convert_fusion.5), channel_id=1, source_target_pairs={{0,8},{2,10},{4,12},{6,14},{8,16},{10,18},{12,20},{14,22},{1,9},{3... | collective-permute-start | bytes 1572872 | tf_op jit(solution)/shard_map/ppermute | solution.py:338
  192.9 12.1 %collective-permute-start.37 = (bf16[16,128,128]{2,1,0:T(8,128)(2,1)S(1)}, bf16[16,128,128]{2,1,0:T(8,128)(2,1)S(1)}, u32[]{:S(2)}, u32[]{:S(2)}) collective-permute-start(bf16[16,128,128]{2,1,0:T(8,128)(2,1)S(1)} %add_convert_fusion.2), channel_id=1, source_target_pairs={{16,8},{18,10},{20,12},{22,14},{24,16},{26,18},{28,20},{30,22},{17... | collective-permute-start | bytes 1572872 | tf_op jit(solution)/shard_map/ppermute | solution.py:338
  193.7 15.0 %collective-permute-start.26 = (bf16[16,128,128]{2,1,0:T(8,128)(2,1)S(1)}, bf16[16,128,128]{2,1,0:T(8,128)(2,1)S(1)}, u32[]{:S(2)}, u32[]{:S(2)}) collective-permute-start(bf16[16,128,128]{2,1,0:T(8,128)(2,1)S(1)} %copy-done.39), channel_id=1, source_target_pairs={{0,4},{2,6},{4,0},{6,2},{8,12},{10,14},{12,8},{14,10},{16,20},{18,... | collective-permute-start | bytes 1572872 | tf_op jit(solution)/shard_map/ppermute | solution.py:343
  200.4 11.2 %collective-permute-start.32 = (bf16[16,128,128]{2,1,0:T(8,128)(2,1)S(1)}, bf16[16,128,128]{2,1,0:T(8,128)(2,1)S(1)}, u32[]{:S(2)}, u32[]{:S(2)}) collective-permute-start(bf16[16,128,128]{2,1,0:T(8,128)(2,1)S(1)} %add_convert_fusion.4), channel_id=1, source_target_pairs={{0,8},{2,10},{4,12},{6,14},{8,16},{10,18},{12,20},{14,22},{16,24},... | collective-permute-start | bytes 1572872 | tf_op jit(solution)/shard_map/ppermute | solution.py:338
  205.1 11.6 %collective-permute-start.38 = (bf16[16,128,128]{2,1,0:T(8,128)(2,1)S(1)}, bf16[16,128,128]{2,1,0:T(8,128)(2,1)S(1)}, u32[]{:S(2)}, u32[]{:S(2)}) collective-permute-start(bf16[16,128,128]{2,1,0:T(8,128)(2,1)S(1)} %add_convert_fusion.1), channel_id=1, source_target_pairs={{8,0},{10,2},{12,4},{14,6},{16,8},{18,10},{20,12},{22,14},{24,16},... | collective-permute-start | bytes 1572872 | tf_op jit(solution)/shard_map/ppermute | solution.py:338
  217.0 55.1 %copy-start.3 = (bf16[16,128,128]{2,1,0:T(8,128)(2,1)}, bf16[16,128,128]{2,1,0:T(8,128)(2,1)S(1)}, u32[]{:S(2)}) copy-start(bf16[16,128,128]{2,1,0:T(8,128)(2,1)S(1)} %add_convert_fusion.refs_0_) | copy-start | bytes 1572868
  217.0 12.2 %collective-permute-start.41 = (bf16[16,128,128]{2,1,0:T(8,128)(2,1)S(1)}, bf16[16,128,128]{2,1,0:T(8,128)(2,1)S(1)}, u32[]{:S(2)}, u32[]{:S(2)}) collective-permute-start(bf16[16,128,128]{2,1,0:T(8,128)(2,1)S(1)} %add_convert_fusion.refs_0_), channel_id=1, source_target_pairs={{8,0},{10,2},{12,4},{14,6},{16,8},{18,10},{20,12},{22,14},{24,16},... | collective-permute-start | bytes 1572872 | tf_op jit(solution)/shard_map/ppermute | solution.py:111
  218.3 12.2 %collective-permute-start.40 = (bf16[16,128,128]{2,1,0:T(8,128)(2,1)S(1)}, bf16[16,128,128]{2,1,0:T(8,128)(2,1)S(1)}, u32[]{:S(2)}, u32[]{:S(2)}) collective-permute-start(bf16[16,128,128]{2,1,0:T(8,128)(2,1)S(1)} %add_convert_fusion.refs_0_), channel_id=1, source_target_pairs={{0,8},{2,10},{4,12},{6,14},{8,16},{10,18},{12,20},{14,22},{16,24},... | collective-permute-start | bytes 1572872 | tf_op jit(solution)/shard_map/ppermute | solution.py:110
  229.2 13.3 %collective-permute-start.45 = (bf16[16,128,128]{2,1,0:T(8,128)(2,1)S(1)}, bf16[16,128,128]{2,1,0:T(8,128)(2,1)S(1)}, u32[]{:S(2)}, u32[]{:S(2)}) collective-permute-start(bf16[16,128,128]{2,1,0:T(8,128)(2,1)S(1)} %collective-permute-done.41.refs_3_), channel_id=1, source_target_pairs={{8,0},{10,2},{12,4},{14,6},{16,8},{18,10},{20,12},{22,14},{9,1},{1... | collective-permute-start | bytes 1572872 | tf_op jit(solution)/shard_map/ppermute | solution.py:111
  230.5 13.3 %collective-permute-start.44 = (bf16[16,128,128]{2,1,0:T(8,128)(2,1)S(1)}, bf16[16,128,128]{2,1,0:T(8,128)(2,1)S(1)}, u32[]{:S(2)}, u32[]{:S(2)}) collective-permute-start(bf16[16,128,128]{2,1,0:T(8,128)(2,1)S(1)} %collective-permute-done.40.refs_2_), channel_id=1, source_target_pairs={{8,16},{10,18},{12,20},{14,22},{16,24},{18,26},{20,28},{22,30},{9,... | collective-permute-start | bytes 1572872 | tf_op jit(solution)/shard_map/ppermute | solution.py:110
  231.2 14.4 %collective-permute-start.39 = (bf16[16,128,128]{2,1,0:T(8,128)(2,1)S(1)}, bf16[16,128,128]{2,1,0:T(8,128)(2,1)S(1)}, u32[]{:S(2)}, u32[]{:S(2)}) collective-permute-start(bf16[16,128,128]{2,1,0:T(8,128)(2,1)S(1)} %add_convert_fusion.refs_0_), channel_id=1, source_target_pairs={{0,4},{2,6},{4,0},{6,2},{8,12},{10,14},{12,8},{14,10},{16,20},{18,... | collective-permute-start | bytes 1572872 | tf_op jit(solution)/shard_map/ppermute | solution.py:107
  232.0 24.8 %collective-permute-start.43 = (bf16[16,128,128]{2,1,0:T(8,128)(2,1)S(1)}, bf16[16,128,128]{2,1,0:T(8,128)(2,1)S(1)}, u32[]{:S(2)}, u32[]{:S(2)}) collective-permute-start(bf16[16,128,128]{2,1,0:T(8,128)(2,1)S(1)} %collective-permute-done.41.refs_3_), channel_id=1, source_target_pairs={{0,4},{2,6},{4,0},{6,2},{8,12},{10,14},{12,8},{14,10},{16,20},{18,... | collective-permute-start | bytes 1572872 | tf_op jit(solution)/shard_map/ppermute | solution.py:115
  242.5 15.0 %collective-permute-start.49 = (bf16[16,128,128]{2,1,0:T(8,128)(2,1)S(1)}, bf16[16,128,128]{2,1,0:T(8,128)(2,1)S(1)}, u32[]{:S(2)}, u32[]{:S(2)}) collective-permute-start(bf16[16,128,128]{2,1,0:T(8,128)(2,1)S(1)} %collective-permute-done.45.refs_7_), channel_id=1, source_target_pairs={{8,0},{10,2},{12,4},{14,6},{9,1},{11,3},{13,5},{15,7}} | collective-permute-start | bytes 1572872 | tf_op jit(solution)/shard_map/ppermute | solution.py:111
  243.8 16.9 %collective-permute-start.48 = (bf16[16,128,128]{2,1,0:T(8,128)(2,1)S(1)}, bf16[16,128,128]{2,1,0:T(8,128)(2,1)S(1)}, u32[]{:S(2)}, u32[]{:S(2)}) collective-permute-start(bf16[16,128,128]{2,1,0:T(8,128)(2,1)S(1)} %collective-permute-done.44.refs_6_), channel_id=1, source_target_pairs={{16,24},{18,26},{20,28},{22,30},{17,25},{19,27},{21,29},{23,31}} | collective-permute-start | bytes 1572872 | tf_op jit(solution)/shard_map/ppermute | solution.py:110
  244.5 17.7 %collective-permute-start.42 = (bf16[16,128,128]{2,1,0:T(8,128)(2,1)S(1)}, bf16[16,128,128]{2,1,0:T(8,128)(2,1)S(1)}, u32[]{:S(2)}, u32[]{:S(2)}) collective-permute-start(bf16[16,128,128]{2,1,0:T(8,128)(2,1)S(1)} %collective-permute-done.40.refs_2_), channel_id=1, source_target_pairs={{8,12},{10,14},{12,8},{14,10},{16,20},{18,22},{20,16},{22,18},{24,... | collective-permute-start | bytes 1572872 | tf_op jit(solution)/shard_map/ppermute | solution.py:114
  245.6 20.1 %collective-permute-start.47 = (bf16[16,128,128]{2,1,0:T(8,128)(2,1)S(1)}, bf16[16,128,128]{2,1,0:T(8,128)(2,1)S(1)}, u32[]{:S(2)}, u32[]{:S(2)}) collective-permute-start(bf16[16,128,128]{2,1,0:T(8,128)(2,1)S(1)} %collective-permute-done.45.refs_7_), channel_id=1, source_target_pairs={{0,4},{2,6},{4,0},{6,2},{8,12},{10,14},{12,8},{14,10},{1,5},{3,7},... | collective-permute-start | bytes 1572872 | tf_op jit(solution)/shard_map/ppermute | solution.py:115
  256.8 8.8 %collective-permute-start.46 = (bf16[16,128,128]{2,1,0:T(8,128)(2,1)S(1)}, bf16[16,128,128]{2,1,0:T(8,128)(2,1)S(1)}, u32[]{:S(2)}, u32[]{:S(2)}) collective-permute-start(bf16[16,128,128]{2,1,0:T(8,128)(2,1)S(1)} %collective-permute-done.44.refs_6_), channel_id=1, source_target_pairs={{16,20},{18,22},{20,16},{22,18},{24,28},{26,30},{28,24},{30,26},{1... | collective-permute-start | bytes 1572872 | tf_op jit(solution)/shard_map/ppermute | solution.py:114
  257.5 13.7 %collective-permute-start.51 = (bf16[16,128,128]{2,1,0:T(8,128)(2,1)S(1)}, bf16[16,128,128]{2,1,0:T(8,128)(2,1)S(1)}, u32[]{:S(2)}, u32[]{:S(2)}) collective-permute-start(bf16[16,128,128]{2,1,0:T(8,128)(2,1)S(1)} %collective-permute-done.49.refs_11_), channel_id=1, source_target_pairs={{0,4},{2,6},{4,0},{6,2},{1,5},{3,7},{5,1},{7,3}} | collective-permute-start | bytes 1572872 | tf_op jit(solution)/shard_map/ppermute | solution.py:115
  260.7 11.4 %collective-permute-start.50 = (bf16[16,128,128]{2,1,0:T(8,128)(2,1)S(1)}, bf16[16,128,128]{2,1,0:T(8,128)(2,1)}, u32[]{:S(2)}, u32[]{:S(2)}) collective-permute-start(bf16[16,128,128]{2,1,0:T(8,128)(2,1)S(1)} %collective-permute-done.48.refs_10_), channel_id=1, source_target_pairs={{24,28},{26,30},{28,24},{30,26},{25,29},{27,31},{29,25},{31,27}} | collective-permute-start | bytes 1572872 | tf_op jit(solution)/shard_map/ppermute | solution.py:114
  282.5 9.5 %collective-permute-start.52 = (f32[2,4,128,128]{3,2,1,0:T(8,128)}, f32[2,4,128,128]{3,2,1,0:T(8,128)S(1)}, u32[]{:S(2)}, u32[]{:S(2)}) collective-permute-start(f32[2,4,128,128]{3,2,1,0:T(8,128)} %get-tuple-element.41), channel_id=1, source_target_pairs={{0,1},{1,0},{2,3},{3,2},{4,5},{5,4},{6,7},{7,6},{8,9},{9,8},{10,11... | collective-permute-start | bytes 1572872 | tf_op jit(solution)/shard_map/ppermute | solution.py:366
  293.1 1.6 collective-permute-start.53
  295.8 1.4 collective-permute-start.54
  297.2 5.6 %collective-permute-start.55 = (f32[128,256]{1,0:T(8,128)S(1)}, f32[128,256]{1,0:T(8,128)S(1)}, u32[]{:S(2)}, u32[]{:S(2)}) collective-permute-start(f32[128,256]{1,0:T(8,128)S(1)} %dynamic-slice_add_fusion), channel_id=1, source_target_pairs={{0,1},{1,0},{2,3},{3,2},{4,5},{5,4},{6,7},{7,6},{8,9},{9,8},{10,11... | collective-permute-start | bytes 393224 | tf_op jit(solution)/shard_map/ppermute | solution.py:354
  302.8 5.0 %collective-permute-start.56 = (f32[128,256]{1,0:T(8,128)S(1)}, f32[128,256]{1,0:T(8,128)S(1)}, u32[]{:S(2)}, u32[]{:S(2)}) collective-permute-start(f32[128,256]{1,0:T(8,128)S(1)} %add.123), channel_id=1, source_target_pairs={{0,4},{2,6},{4,0},{6,2},{8,12},{10,14},{12,8},{14,10},{16,20},{18,... | collective-permute-start | bytes 393224 | tf_op jit(solution)/shard_map/ppermute | solution.py:355
  307.9 9.9 %collective-permute-start.57 = (f32[128,256]{1,0:T(8,128)S(1)}, f32[128,256]{1,0:T(8,128)S(1)}, u32[]{:S(2)}, u32[]{:S(2)}) collective-permute-start(f32[128,256]{1,0:T(8,128)S(1)} %add.124), channel_id=1, source_target_pairs={{0,8},{2,10},{4,12},{6,14},{8,0},{10,2},{12,4},{14,6},{16,24},{18,... | collective-permute-start | bytes 393224 | tf_op jit(solution)/shard_map/ppermute | solution.py:358
  317.8 5.9 %collective-permute-start.58 = (f32[128,256]{1,0:T(8,128)S(1)}, f32[128,256]{1,0:T(8,128)S(1)}, u32[]{:S(2)}, u32[]{:S(2)}) collective-permute-start(f32[128,256]{1,0:T(8,128)S(1)} %add.125), channel_id=1, source_target_pairs={{0,16},{2,18},{4,20},{6,22},{8,24},{10,26},{12,28},{14,30},{16,0},... | collective-permute-start | bytes 393224 | tf_op jit(solution)/shard_map/ppermute | solution.py:358
  323.8 1.4 collective-permute-start.59
  (39 other events, 677.7 us)

commit v2 on v1

--- a/solution.py
+++ b/solution.py
@@ -74,6 +74,7 @@
         in_specs=[VMEM],
         out_specs=[VMEM] * 2,
         scratch_shapes=[pltpu.VMEM((n, 2 * n), F32)],
+        compiler_params=pltpu.CompilerParams(vmem_limit_bytes=4 << 20),
         name="factor",
     )(gram)
 
@@ -214,6 +215,7 @@
             pltpu.SemaphoreType.DMA((len(found),)),
             pltpu.SemaphoreType.DMA((4,)),
         ],
+        compiler_params=pltpu.CompilerParams(vmem_limit_bytes=12 << 20),
         name="forward",
     )(*codes, *values, *[chunk for _, _, chunk in found])
 
@@ -314,6 +316,7 @@
             pltpu.SemaphoreType.DMA((len(where),)),
             pltpu.SemaphoreType.DMA((len(where),)),
         ],
+        compiler_params=pltpu.CompilerParams(vmem_limit_bytes=20 << 20),
         name="backward",
     )(*codes, *values, near, far)
     return dict(zip(where, outs[: len(where)])), dict(zip(where, outs[len(where) :]))

time: 341 us -> 316 us (0.927)
  Pallas kernels: 54.1 us -> 40.9 us
  starting transfers between devices: 108 us -> 102 us
  other arithmetic: 6.62 us -> 1.77 us
  waiting for transfers between devices: 158 us -> 162 us
  local copies, waits for them, and re-layouts: 5.16 us -> 1.36 us
    pallas_call x2, Pallas kernels: 19.3 us -> 12.1 us  [forward(): pl.pallas_call(functools.partial(forward_kernel, grid.nz, [spot[:2] for s...]
    pallas_call x1, Pallas kernels: 10.9 us -> 6.96 us  [backward(): pl.pallas_call(functools.partial(backward_kernel, nz, where), out_shape=[...]
    ppermute x6, waiting for transfers between devices: 30.1 us -> 34 us  [gather_chips(): move(falling, perm=grid.along_y(lambda z: z <= nz - 1 - d))]
    unnamed x86 -> x8, local copies, waits for them, and re-layouts: 3.82 us -> 0.02 us
  transfers between devices with their start and end apart: 60 -> 60, of which waited for: 39 -> 38; matrix products, arithmetic and copies ran while one was open for 1% -> 0% of each run, Pallas kernels for 0% -> 0%
where the time goes in v2:
time: 316 us; the launch traced here: 315 us
  waiting for transfers between devices  162 us (51%)
  starting transfers between devices  102 us (32%)
  Pallas kernels  40.9 us (13%)
  matrix products  4.07 us (1%)
    ppermute x6, waiting for transfers between devices, gather_chips(): move(falling, perm=grid.along_y(lambda z: z <= nz - 1 - d))  34 us
    ppermute x6, waiting for transfers between devices, gather_chips(): falling = move(falling, perm=grid.down(lambda z: z <= nz - d))  33.4 us
    pallas_call x2, Pallas kernels, factor(): pl.pallas_call(functools.partial(factor_kernel, 1.0 / cells), out_shape=[...  21.8 us
    ppermute x6, waiting for transfers between devices, scatter_chips(): move(sends[sign * d], perm=grid.along_y(inside)).astype(F32)  20.4 us
    ppermute x6, starting transfers between devices, gather_chips(): move(falling, perm=grid.along_y(lambda z: z <= nz - 1 - d))  19.4 us
    ppermute x2, waiting for transfers between devices, whole_rows(): part = (keep + lax.ppermute(send, 'gene', grid.swap)).reshape(2, -1, HALF)  18.2 us
    ppermute x4, starting transfers between devices, sum_gram(): total = total + move(total, perm=[(s, s ^ 4 * step) for s in range(grid.n)])  18.1 us
    ppermute x6, starting transfers between devices, gather_chips(): rising = move(rising, perm=grid.up(lambda z: z >= d - 1))  12.9 us
  transfers between devices with their start and end apart: 60, of which 38 were waited for; matrix products, arithmetic and copies ran while one was open for 0% of the time, Pallas kernels for 0%

profile of v2, /device:TPU:0, one launch (start us, length us, event | category | flops | bytes accessed | tf_op | source)
XLA Modules:
  0.0 315.0 jit_solution(6575743512410661794)
XLA Ops:
  4.9 5.5 %collective-permute-start.4 = (bf16[16,128,128]{2,1,0:T(8,128)(2,1)S(1)}, bf16[16,128,128]{2,1,0:T(8,128)(2,1)S(1)}, u32[]{:S(2)}, u32[]{:S(2)}) collective-permute-start(bf16[16,128,128]{2,1,0:T(8,128)(2,1)S(1)} %bitcast.17), channel_id=1, source_target_pairs={{0,8},{2,10},{4,12},{6,14},{8,16},{10,18},{12,20},{14,22},{16,24},... | collective-permute-start | bytes 1572872 | tf_op jit(solution)/shard_map/ppermute | solution.py:111
  10.5 2.0 collective-permute-start.3
  12.6 8.1 %collective-permute-done.5.refs_3_ = bf16[16,128,128]{2,1,0:T(8,128)(2,1)S(1)} collective-permute-done((bf16[16,128,128]{2,1,0:T(8,128)(2,1)S(1)}, bf16[16,128,128]{2,1,0:T(8,128)(2,1)S(1)}, u32[]{:S(2)}, u32[]{:S(2)}) %collective-permute-start.5) | collective-permute-done | bytes 524320 | tf_op jit(solution)/shard_map/ppermute | solution.py:112
  24.6 3.6 %collective-permute-start.7 = (bf16[16,128,128]{2,1,0:T(8,128)(2,1)S(1)}, bf16[16,128,128]{2,1,0:T(8,128)(2,1)S(1)}, u32[]{:S(2)}, u32[]{:S(2)}) collective-permute-start(bf16[16,128,128]{2,1,0:T(8,128)(2,1)S(1)} %collective-permute-done.5.refs_3_), channel_id=1, source_target_pairs={{0,4},{2,6},{4,0},{6,2},{8,12},{10,14},{12,8},{14,10},{16,20},{18,... | collective-permute-start | bytes 1572872 | tf_op jit(solution)/shard_map/ppermute | solution.py:116
  28.9 7.1 %collective-permute-done.9.refs_7_ = bf16[16,128,128]{2,1,0:T(8,128)(2,1)S(1)} collective-permute-done((bf16[16,128,128]{2,1,0:T(8,128)(2,1)S(1)}, bf16[16,128,128]{2,1,0:T(8,128)(2,1)S(1)}, u32[]{:S(2)}, u32[]{:S(2)}) %collective-permute-start.9) | collective-permute-done | bytes 524320 | tf_op jit(solution)/shard_map/ppermute | solution.py:112
  38.0 2.5 collective-permute-done.7.refs_5_
  40.5 3.6 %collective-permute-start.11 = (bf16[16,128,128]{2,1,0:T(8,128)(2,1)S(1)}, bf16[16,128,128]{2,1,0:T(8,128)(2,1)S(1)}, u32[]{:S(2)}, u32[]{:S(2)}) collective-permute-start(bf16[16,128,128]{2,1,0:T(8,128)(2,1)S(1)} %collective-permute-done.9.refs_7_), channel_id=1, source_target_pairs={{0,4},{2,6},{4,0},{6,2},{8,12},{10,14},{12,8},{14,10},{1,5},{3,7},... | collective-permute-start | bytes 1572872 | tf_op jit(solution)/shard_map/ppermute | solution.py:116
  44.8 5.6 %collective-permute-done.13.refs_11_ = bf16[16,128,128]{2,1,0:T(8,128)(2,1)S(1)} collective-permute-done((bf16[16,128,128]{2,1,0:T(8,128)(2,1)S(1)}, bf16[16,128,128]{2,1,0:T(8,128)(2,1)S(1)}, u32[]{:S(2)}, u32[]{:S(2)}) %collective-permute-start.13) | collective-permute-done | bytes 524320 | tf_op jit(solution)/shard_map/ppermute | solution.py:112
  50.4 3.0 collective-permute-start.15
  54.1 3.0 collective-permute-done.11.refs_9_
  57.2 9.6 %collective-permute-done.15.refs_13_ = bf16[16,128,128]{2,1,0:T(8,128)(2,1)S(1)} collective-permute-done((bf16[16,128,128]{2,1,0:T(8,128)(2,1)S(1)}, bf16[16,128,128]{2,1,0:T(8,128)(2,1)S(1)}, u32[]{:S(2)}, u32[]{:S(2)}) %collective-permute-start.15) | collective-permute-done | bytes 524320 | tf_op jit(solution)/shard_map/ppermute | solution.py:116
  66.7 5.3 %forward.2 = (f32[2,4,128,128]{3,2,1,0:T(8,128)S(1)}, f32[2,4,128,128]{3,2,1,0:T(8,128)S(1)}) custom-call(s32[64]{0:T(128)S(1)} %fusion.8.own_code, s32[64]{0:T(128)S(1)} %collective-permute-done.other_code, bf16[64,128,128]{2,1,0:T(8,128)(2,1)S(1)} %copy-done, bf16[64,128,128]{2,1,0:T(8,128)(2,1)S(1)} %collective-permute-done.1.other_hbm, ...), custom_call_target="tpu_custom_call" | custom-call | tf_op jit(solution)/shard_map/forward/pallas_call | solution.py:205
  72.1 1.7 collective-permute-start.16
  73.8 10.6 %collective-permute-done.16 = f32[2,4,128,128]{3,2,1,0:T(8,128)S(1)} collective-permute-done((f32[2,4,128,128]{3,2,1,0:T(8,128)S(1)}, f32[2,4,128,128]{3,2,1,0:T(8,128)S(1)}, u32[]{:S(2)}, u32[]{:S(2)}) %collective-permute-start.16) | collective-permute-done | bytes 524320 | tf_op jit(solution)/shard_map/ppermute | solution.py:369
  84.6 1.5 collective-permute-done.17
  88.6 1.7 collective-permute-start.19
  90.4 3.9 %collective-permute-done.19 = f32[128,256]{1,0:T(8,128)S(1)} collective-permute-done((f32[128,256]{1,0:T(8,128)S(1)}, f32[128,256]{1,0:T(8,128)S(1)}, u32[]{:S(2)}, u32[]{:S(2)}) %collective-permute-start.19) | collective-permute-done | bytes 131104 | tf_op jit(solution)/shard_map/ppermute | solution.py:357
  94.3 1.8 collective-permute-start.20
  96.1 3.2 %collective-permute-done.20 = f32[128,256]{1,0:T(8,128)S(1)} collective-permute-done((f32[128,256]{1,0:T(8,128)S(1)}, f32[128,256]{1,0:T(8,128)S(1)}, u32[]{:S(2)}, u32[]{:S(2)}) %collective-permute-start.20) | collective-permute-done | bytes 131104 | tf_op jit(solution)/shard_map/ppermute | solution.py:358
  99.3 2.9 collective-permute-start.21
  102.2 2.9 collective-permute-done.21
  105.2 6.7 %collective-permute-start.22 = (f32[128,256]{1,0:T(8,128)S(1)}, f32[128,256]{1,0:T(8,128)S(1)}, u32[]{:S(2)}, u32[]{:S(2)}) collective-permute-start(f32[128,256]{1,0:T(8,128)S(1)} %add.106), channel_id=1, source_target_pairs={{0,16},{2,18},{4,20},{6,22},{8,24},{10,26},{12,28},{14,30},{16,0},... | collective-permute-start | bytes 393224 | tf_op jit(solution)/shard_map/ppermute | solution.py:361
  111.9 3.3 %collective-permute-done.22 = f32[128,256]{1,0:T(8,128)S(1)} collective-permute-done((f32[128,256]{1,0:T(8,128)S(1)}, f32[128,256]{1,0:T(8,128)S(1)}, u32[]{:S(2)}, u32[]{:S(2)}) %collective-permute-start.22) | collective-permute-done | bytes 131104 | tf_op jit(solution)/shard_map/ppermute | solution.py:361
  115.3 1.3 collective-permute-done.23
  116.7 10.9 %factor.2 = (f32[256,256]{1,0:T(8,128)}, f32[256,256]{1,0:T(8,128)S(1)}) custom-call(f32[256,256]{1,0:T(8,128)S(1)} %maximum_select_fusion.6.gram_ref), custom_call_target="tpu_custom_call" | custom-call | tf_op jit(solution)/shard_map/factor/pallas_call | solution.py:71
  129.7 1.6 collective-permute-start.25
  131.2 6.9 %collective-permute-done.25.far_hbm = bf16[2,128,512]{2,1,0:T(8,128)(2,1)S(1)} collective-permute-done((bf16[2,128,512]{2,1,0:T(8,128)(2,1)S(1)}, bf16[2,128,512]{2,1,0:T(8,128)(2,1)S(1)}, u32[]{:S(2)}, u32[]{:S(2)}) %collective-permute-start.25) | collective-permute-done | bytes 262176 | tf_op jit(solution)/shard_map/ppermute | solution.py:401
  138.1 7.0 %backward.1 = (f32[16,128,128]{2,1,0:T(8,128)S(1)}, f32[16,128,128]{2,1,0:T(8,128)S(1)}, f32[16,128,128]{2,1,0:T(8,128)S(1)}, f32[16,128,128]{2,1,0:T(8,128)S(1)...) custom-call(s32[64]{0:T(128)S(1)} %fusion.8.own_code, ...), custom_call_target="tpu_custom_call" | custom-call | tf_op jit(solution)/shard_map/backward/pallas_call | solution.py:304
  145.1 3.4 %collective-permute-start.29 = (bf16[16,128,128]{2,1,0:T(8,128)(2,1)S(1)}, bf16[16,128,128]{2,1,0:T(8,128)(2,1)S(1)}, u32[]{:S(2)}, u32[]{:S(2)}) collective-permute-start(bf16[16,128,128]{2,1,0:T(8,128)(2,1)S(1)} %get-tuple-element.33), channel_id=1, source_target_pairs={{0,4},{2,6},{4,0},{6,2},{1,5},{3,7},{5,1},{7,3}} | collective-permute-start | bytes 1572872 | tf_op jit(solution)/shard_map/ppermute | solution.py:337
  149.2 2.4 collective-permute-start.28
  151.6 10.1 %collective-permute-done.29 = bf16[16,128,128]{2,1,0:T(8,128)(2,1)S(1)} collective-permute-done((bf16[16,128,128]{2,1,0:T(8,128)(2,1)S(1)}, bf16[16,128,128]{2,1,0:T(8,128)(2,1)S(1)}, u32[]{:S(2)}, u32[]{:S(2)}) %collective-permute-start.29) | collective-permute-done | bytes 524320 | tf_op jit(solution)/shard_map/ppermute | solution.py:337
  164.8 3.4 %collective-permute-start.27 = (bf16[16,128,128]{2,1,0:T(8,128)(2,1)S(1)}, bf16[16,128,128]{2,1,0:T(8,128)(2,1)S(1)}, u32[]{:S(2)}, u32[]{:S(2)}) collective-permute-start(bf16[16,128,128]{2,1,0:T(8,128)(2,1)S(1)} %get-tuple-element.29), channel_id=1, source_target_pairs={{0,4},{2,6},{4,0},{6,2},{8,12},{10,14},{12,8},{14,10},{16,20},{18,... | collective-permute-start | bytes 1572872 | tf_op jit(solution)/shard_map/ppermute | solution.py:337
  168.2 4.7 %collective-permute-done.28 = bf16[16,128,128]{2,1,0:T(8,128)(2,1)S(1)} collective-permute-done((bf16[16,128,128]{2,1,0:T(8,128)(2,1)S(1)}, bf16[16,128,128]{2,1,0:T(8,128)(2,1)S(1)}, u32[]{:S(2)}, u32[]{:S(2)}) %collective-permute-start.28) | collective-permute-done | bytes 524320 | tf_op jit(solution)/shard_map/ppermute | solution.py:337
  173.9 2.3 collective-permute-start.31
  177.2 1.6 collective-permute-start.26
  178.7 5.5 %collective-permute-done.27 = bf16[16,128,128]{2,1,0:T(8,128)(2,1)S(1)} collective-permute-done((bf16[16,128,128]{2,1,0:T(8,128)(2,1)S(1)}, bf16[16,128,128]{2,1,0:T(8,128)(2,1)S(1)}, u32[]{:S(2)}, u32[]{:S(2)}) %collective-permute-start.27) | collective-permute-done | bytes 524320 | tf_op jit(solution)/shard_map/ppermute | solution.py:337
  184.4 3.9 %collective-permute-start.32 = (bf16[16,128,128]{2,1,0:T(8,128)(2,1)S(1)}, bf16[16,128,128]{2,1,0:T(8,128)(2,1)S(1)}, u32[]{:S(2)}, u32[]{:S(2)}) collective-permute-start(bf16[16,128,128]{2,1,0:T(8,128)(2,1)S(1)} %add_convert_fusion.4), channel_id=1, source_target_pairs={{0,8},{2,10},{4,12},{6,14},{8,16},{10,18},{12,20},{14,22},{16,24},... | collective-permute-start | bytes 1572872 | tf_op jit(solution)/shard_map/ppermute | solution.py:341
  189.9 3.9 %collective-permute-done.26 = bf16[16,128,128]{2,1,0:T(8,128)(2,1)S(1)} collective-permute-done((bf16[16,128,128]{2,1,0:T(8,128)(2,1)S(1)}, bf16[16,128,128]{2,1,0:T(8,128)(2,1)S(1)}, u32[]{:S(2)}, u32[]{:S(2)}) %collective-permute-start.26) | collective-permute-done | bytes 524320 | tf_op jit(solution)/shard_map/ppermute | solution.py:346
  195.0 4.6 %collective-permute-done.38 = bf16[16,128,128]{2,1,0:T(8,128)(2,1)S(1)} collective-permute-done((bf16[16,128,128]{2,1,0:T(8,128)(2,1)S(1)}, bf16[16,128,128]{2,1,0:T(8,128)(2,1)S(1)}, u32[]{:S(2)}, u32[]{:S(2)}) %collective-permute-start.38) | collective-permute-done | bytes 524320 | tf_op jit(solution)/shard_map/ppermute | solution.py:341
  201.2 4.6 %collective-permute-start.40 = (bf16[16,128,128]{2,1,0:T(8,128)(2,1)S(1)}, bf16[16,128,128]{2,1,0:T(8,128)(2,1)S(1)}, u32[]{:S(2)}, u32[]{:S(2)}) collective-permute-start(bf16[16,128,128]{2,1,0:T(8,128)(2,1)S(1)} %add_convert_fusion.refs_0_), channel_id=1, source_target_pairs={{0,8},{2,10},{4,12},{6,14},{8,16},{10,18},{12,20},{14,22},{16,24},... | collective-permute-start | bytes 1572872 | tf_op jit(solution)/shard_map/ppermute | solution.py:111
  205.8 6.0 %collective-permute-done.41.refs_3_ = bf16[16,128,128]{2,1,0:T(8,128)(2,1)S(1)} collective-permute-done((bf16[16,128,128]{2,1,0:T(8,128)(2,1)S(1)}, bf16[16,128,128]{2,1,0:T(8,128)(2,1)S(1)}, u32[]{:S(2)}, u32[]{:S(2)}) %collective-permute-start.41) | collective-permute-done | bytes 524320 | tf_op jit(solution)/shard_map/ppermute | solution.py:112
  213.8 1.6 collective-permute-start.39
  215.4 2.4 collective-permute-start.43
  217.8 6.6 %collective-permute-done.45.refs_7_ = bf16[16,128,128]{2,1,0:T(8,128)(2,1)S(1)} collective-permute-done((bf16[16,128,128]{2,1,0:T(8,128)(2,1)S(1)}, bf16[16,128,128]{2,1,0:T(8,128)(2,1)S(1)}, u32[]{:S(2)}, u32[]{:S(2)}) %collective-permute-start.45) | collective-permute-done | bytes 524320 | tf_op jit(solution)/shard_map/ppermute | solution.py:112
  227.1 1.5 collective-permute-done.39.refs_1_
  228.7 3.4 %collective-permute-start.47 = (bf16[16,128,128]{2,1,0:T(8,128)(2,1)S(1)}, bf16[16,128,128]{2,1,0:T(8,128)(2,1)S(1)}, u32[]{:S(2)}, u32[]{:S(2)}) collective-permute-start(bf16[16,128,128]{2,1,0:T(8,128)(2,1)S(1)} %collective-permute-done.45.refs_7_), channel_id=1, source_target_pairs={{0,4},{2,6},{4,0},{6,2},{8,12},{10,14},{12,8},{14,10},{1,5},{3,7},... | collective-permute-start | bytes 1572872 | tf_op jit(solution)/shard_map/ppermute | solution.py:116
  232.1 7.8 %collective-permute-done.43.refs_5_ = bf16[16,128,128]{2,1,0:T(8,128)(2,1)S(1)} collective-permute-done((bf16[16,128,128]{2,1,0:T(8,128)(2,1)S(1)}, bf16[16,128,128]{2,1,0:T(8,128)(2,1)S(1)}, u32[]{:S(2)}, u32[]{:S(2)}) %collective-permute-start.43) | collective-permute-done | bytes 524320 | tf_op jit(solution)/shard_map/ppermute | solution.py:116
  240.6 3.4 %collective-permute-start.51 = (bf16[16,128,128]{2,1,0:T(8,128)(2,1)S(1)}, bf16[16,128,128]{2,1,0:T(8,128)(2,1)S(1)}, u32[]{:S(2)}, u32[]{:S(2)}) collective-permute-start(bf16[16,128,128]{2,1,0:T(8,128)(2,1)S(1)} %collective-permute-done.49.refs_11_), channel_id=1, source_target_pairs={{0,4},{2,6},{4,0},{6,2},{1,5},{3,7},{5,1},{7,3}} | collective-permute-start | bytes 1572872 | tf_op jit(solution)/shard_map/ppermute | solution.py:116
  244.8 5.5 %collective-permute-done.47.refs_9_ = bf16[16,128,128]{2,1,0:T(8,128)(2,1)S(1)} collective-permute-done((bf16[16,128,128]{2,1,0:T(8,128)(2,1)S(1)}, bf16[16,128,128]{2,1,0:T(8,128)(2,1)S(1)}, u32[]{:S(2)}, u32[]{:S(2)}) %collective-permute-start.47) | collective-permute-done | bytes 524320 | tf_op jit(solution)/shard_map/ppermute | solution.py:116
  250.2 5.6 %collective-permute-done.51.refs_13_ = bf16[16,128,128]{2,1,0:T(8,128)(2,1)S(1)} collective-permute-done((bf16[16,128,128]{2,1,0:T(8,128)(2,1)S(1)}, bf16[16,128,128]{2,1,0:T(8,128)(2,1)S(1)}, u32[]{:S(2)}, u32[]{:S(2)}) %collective-permute-start.51) | collective-permute-done | bytes 524320 | tf_op jit(solution)/shard_map/ppermute | solution.py:116
  255.8 6.8 %forward.3 = (f32[2,4,128,128]{3,2,1,0:T(8,128)S(1)}, f32[2,4,128,128]{3,2,1,0:T(8,128)S(1)}) custom-call(s32[64]{0:T(128)S(1)} %fusion.8.own_code, s32[64]{0:T(128)S(1)} %collective-permute-done.other_code, bf16[64,128,128]{2,1,0:T(8,128)(2,1)S(1)} %copy-done, bf16[64,128,128]{2,1,0:T(8,128)(2,1)S(1)} %copy-done.2, ...), custom_call_target="tpu_custom_call" | custom-call | tf_op jit(solution)/shard_map/forward/pallas_call | solution.py:205
  262.7 1.6 collective-permute-start.52
  264.3 7.6 %collective-permute-done.52 = f32[2,4,128,128]{3,2,1,0:T(8,128)S(1)} collective-permute-done((f32[2,4,128,128]{3,2,1,0:T(8,128)S(1)}, f32[2,4,128,128]{3,2,1,0:T(8,128)S(1)}, u32[]{:S(2)}, u32[]{:S(2)}) %collective-permute-start.52) | collective-permute-done | bytes 524320 | tf_op jit(solution)/shard_map/ppermute | solution.py:369
  272.1 1.5 collective-permute-done.53
  276.1 1.6 collective-permute-start.55
  277.7 4.0 %collective-permute-done.55 = f32[128,256]{1,0:T(8,128)S(1)} collective-permute-done((f32[128,256]{1,0:T(8,128)S(1)}, f32[128,256]{1,0:T(8,128)S(1)}, u32[]{:S(2)}, u32[]{:S(2)}) %collective-permute-start.55) | collective-permute-done | bytes 131104 | tf_op jit(solution)/shard_map/ppermute | solution.py:357
  281.7 1.7 collective-permute-start.56
  283.4 3.3 %collective-permute-done.56 = f32[128,256]{1,0:T(8,128)S(1)} collective-permute-done((f32[128,256]{1,0:T(8,128)S(1)}, f32[128,256]{1,0:T(8,128)S(1)}, u32[]{:S(2)}, u32[]{:S(2)}) %collective-permute-start.56) | collective-permute-done | bytes 131104 | tf_op jit(solution)/shard_map/ppermute | solution.py:358
  286.8 5.4 %collective-permute-start.57 = (f32[128,256]{1,0:T(8,128)S(1)}, f32[128,256]{1,0:T(8,128)S(1)}, u32[]{:S(2)}, u32[]{:S(2)}) collective-permute-start(f32[128,256]{1,0:T(8,128)S(1)} %add.124), channel_id=1, source_target_pairs={{0,8},{2,10},{4,12},{6,14},{8,0},{10,2},{12,4},{14,6},{16,24},{18,... | collective-permute-start | bytes 393224 | tf_op jit(solution)/shard_map/ppermute | solution.py:361
  292.2 2.9 collective-permute-done.57
  295.2 3.1 collective-permute-start.58
  298.3 3.0 collective-permute-done.58
  302.7 10.9 %factor.3 = (f32[256,256]{1,0:T(8,128)}, f32[256,256]{1,0:T(8,128)S(1)}) custom-call(f32[256,256]{1,0:T(8,128)S(1)} %maximum_select_fusion.7.gram_ref), custom_call_target="tpu_custom_call" | custom-call | tf_op jit(solution)/shard_map/factor/pallas_call | solution.py:71
  313.6 1.4 fusion
  (103 shorter events, 36.6 us)
Async XLA Ops:
  0.6 9.8 %copy-start = (bf16[64,128,128]{2,1,0:T(8,128)(2,1)S(1)}, bf16[64,128,128]{2,1,0:T(8,128)(2,1)}, u32[]{:S(2)}) copy-start(bf16[64,128,128]{2,1,0:T(8,128)(2,1)} %own_hbm.5) | copy-start | bytes 6291460
  0.6 22.7 %copy-start.3 = (s32[64,2]{0,1:T(2,128)S(1)}, s32[64,2]{0,1:T(2,128)}, u32[]{:S(2)}) copy-start(s32[64,2]{0,1:T(2,128)} %param.5) | copy-start | bytes 1540
  1.9 1.7 collective-permute-start.2
  3.6 17.1 %collective-permute-start.5 = (bf16[16,128,128]{2,1,0:T(8,128)(2,1)S(1)}, bf16[16,128,128]{2,1,0:T(8,128)(2,1)S(1)}, u32[]{:S(2)}, u32[]{:S(2)}) collective-permute-start(bf16[16,128,128]{2,1,0:T(8,128)(2,1)S(1)} %bitcast.16), channel_id=1, source_target_pairs={{8,0},{10,2},{12,4},{14,6},{16,8},{18,10},{20,12},{22,14},{24,16},... | collective-permute-start | bytes 1572872 | tf_op jit(solution)/shard_map/ppermute | solution.py:112
  4.9 17.1 %collective-permute-start.4 = (bf16[16,128,128]{2,1,0:T(8,128)(2,1)S(1)}, bf16[16,128,128]{2,1,0:T(8,128)(2,1)S(1)}, u32[]{:S(2)}, u32[]{:S(2)}) collective-permute-start(bf16[16,128,128]{2,1,0:T(8,128)(2,1)S(1)} %bitcast.17), channel_id=1, source_target_pairs={{0,8},{2,10},{4,12},{6,14},{8,16},{10,18},{12,20},{14,22},{16,24},... | collective-permute-start | bytes 1572872 | tf_op jit(solution)/shard_map/ppermute | solution.py:111
  10.5 46.7 %collective-permute-start.1 = (bf16[64,128,128]{2,1,0:T(8,128)(2,1)S(1)}, bf16[64,128,128]{2,1,0:T(8,128)(2,1)S(1)}, u32[]{:S(2)}, u32[]{:S(2)}) collective-permute-start(bf16[64,128,128]{2,1,0:T(8,128)(2,1)S(1)} %copy-done), channel_id=1, source_target_pairs={{0,2},{2,0},{4,6},{6,4},{8,10},{10,8},{12,14},{14,12},{16,18},{18,... | collective-permute-start | bytes 6291464 | tf_op jit(solution)/shard_map/ppermute | solution.py:386
  10.5 17.6 %collective-permute-start.3 = (bf16[16,128,128]{2,1,0:T(8,128)(2,1)S(1)}, bf16[16,128,128]{2,1,0:T(8,128)(2,1)S(1)}, u32[]{:S(2)}, u32[]{:S(2)}) collective-permute-start(bf16[16,128,128]{2,1,0:T(8,128)(2,1)S(1)} %bitcast.18), channel_id=1, source_target_pairs={{0,4},{2,6},{4,0},{6,2},{8,12},{10,14},{12,8},{14,10},{16,20},{18,... | collective-permute-start | bytes 1572872 | tf_op jit(solution)/shard_map/ppermute | solution.py:108
  20.7 15.3 %collective-permute-start.9 = (bf16[16,128,128]{2,1,0:T(8,128)(2,1)S(1)}, bf16[16,128,128]{2,1,0:T(8,128)(2,1)S(1)}, u32[]{:S(2)}, u32[]{:S(2)}) collective-permute-start(bf16[16,128,128]{2,1,0:T(8,128)(2,1)S(1)} %collective-permute-done.5.refs_3_), channel_id=1, source_target_pairs={{8,0},{10,2},{12,4},{14,6},{16,8},{18,10},{20,12},{22,14},{9,1},{1... | collective-permute-start | bytes 1572872 | tf_op jit(solution)/shard_map/ppermute | solution.py:112
  22.0 15.3 %collective-permute-start.8 = (bf16[16,128,128]{2,1,0:T(8,128)(2,1)S(1)}, bf16[16,128,128]{2,1,0:T(8,128)(2,1)S(1)}, u32[]{:S(2)}, u32[]{:S(2)}) collective-permute-start(bf16[16,128,128]{2,1,0:T(8,128)(2,1)S(1)} %collective-permute-done.4.refs_2_), channel_id=1, source_target_pairs={{8,16},{10,18},{12,20},{14,22},{16,24},{18,26},{20,28},{22,30},{9,... | collective-permute-start | bytes 1572872 | tf_op jit(solution)/shard_map/ppermute | solution.py:111
  23.4 1.2 collective-permute-start
  24.6 15.9 %collective-permute-start.7 = (bf16[16,128,128]{2,1,0:T(8,128)(2,1)S(1)}, bf16[16,128,128]{2,1,0:T(8,128)(2,1)S(1)}, u32[]{:S(2)}, u32[]{:S(2)}) collective-permute-start(bf16[16,128,128]{2,1,0:T(8,128)(2,1)S(1)} %collective-permute-done.5.refs_3_), channel_id=1, source_target_pairs={{0,4},{2,6},{4,0},{6,2},{8,12},{10,14},{12,8},{14,10},{16,20},{18,... | collective-permute-start | bytes 1572872 | tf_op jit(solution)/shard_map/ppermute | solution.py:116
  28.2 15.9 %collective-permute-start.6 = (bf16[16,128,128]{2,1,0:T(8,128)(2,1)S(1)}, bf16[16,128,128]{2,1,0:T(8,128)(2,1)S(1)}, u32[]{:S(2)}, u32[]{:S(2)}) collective-permute-start(bf16[16,128,128]{2,1,0:T(8,128)(2,1)S(1)} %collective-permute-done.4.refs_2_), channel_id=1, source_target_pairs={{8,12},{10,14},{12,8},{14,10},{16,20},{18,22},{20,16},{22,18},{24,... | collective-permute-start | bytes 1572872 | tf_op jit(solution)/shard_map/ppermute | solution.py:115
  36.0 14.4 %collective-permute-start.13 = (bf16[16,128,128]{2,1,0:T(8,128)(2,1)S(1)}, bf16[16,128,128]{2,1,0:T(8,128)(2,1)S(1)}, u32[]{:S(2)}, u32[]{:S(2)}) collective-permute-start(bf16[16,128,128]{2,1,0:T(8,128)(2,1)S(1)} %collective-permute-done.9.refs_7_), channel_id=1, source_target_pairs={{8,0},{10,2},{12,4},{14,6},{9,1},{11,3},{13,5},{15,7}} | collective-permute-start | bytes 1572872 | tf_op jit(solution)/shard_map/ppermute | solution.py:112
  37.3 16.1 %collective-permute-start.12 = (bf16[16,128,128]{2,1,0:T(8,128)(2,1)S(1)}, bf16[16,128,128]{2,1,0:T(8,128)(2,1)S(1)}, u32[]{:S(2)}, u32[]{:S(2)}) collective-permute-start(bf16[16,128,128]{2,1,0:T(8,128)(2,1)S(1)} %collective-permute-done.8.refs_6_), channel_id=1, source_target_pairs={{16,24},{18,26},{20,28},{22,30},{17,25},{19,27},{21,29},{23,31}} | collective-permute-start | bytes 1572872 | tf_op jit(solution)/shard_map/ppermute | solution.py:111
  40.5 16.7 %collective-permute-start.11 = (bf16[16,128,128]{2,1,0:T(8,128)(2,1)S(1)}, bf16[16,128,128]{2,1,0:T(8,128)(2,1)S(1)}, u32[]{:S(2)}, u32[]{:S(2)}) collective-permute-start(bf16[16,128,128]{2,1,0:T(8,128)(2,1)S(1)} %collective-permute-done.9.refs_7_), channel_id=1, source_target_pairs={{0,4},{2,6},{4,0},{6,2},{8,12},{10,14},{12,8},{14,10},{1,5},{3,7},... | collective-permute-start | bytes 1572872 | tf_op jit(solution)/shard_map/ppermute | solution.py:116
  44.1 13.1 %collective-permute-start.10 = (bf16[16,128,128]{2,1,0:T(8,128)(2,1)S(1)}, bf16[16,128,128]{2,1,0:T(8,128)(2,1)S(1)}, u32[]{:S(2)}, u32[]{:S(2)}) collective-permute-start(bf16[16,128,128]{2,1,0:T(8,128)(2,1)S(1)} %collective-permute-done.8.refs_6_), channel_id=1, source_target_pairs={{16,20},{18,22},{20,16},{22,18},{24,28},{26,30},{28,24},{30,26},{1... | collective-permute-start | bytes 1572872 | tf_op jit(solution)/shard_map/ppermute | solution.py:115
  50.4 16.3 %collective-permute-start.15 = (bf16[16,128,128]{2,1,0:T(8,128)(2,1)S(1)}, bf16[16,128,128]{2,1,0:T(8,128)(2,1)S(1)}, u32[]{:S(2)}, u32[]{:S(2)}) collective-permute-start(bf16[16,128,128]{2,1,0:T(8,128)(2,1)S(1)} %collective-permute-done.13.refs_11_), channel_id=1, source_target_pairs={{0,4},{2,6},{4,0},{6,2},{1,5},{3,7},{5,1},{7,3}} | collective-permute-start | bytes 1572872 | tf_op jit(solution)/shard_map/ppermute | solution.py:116
  53.4 13.3 %collective-permute-start.14 = (bf16[16,128,128]{2,1,0:T(8,128)(2,1)S(1)}, bf16[16,128,128]{2,1,0:T(8,128)(2,1)S(1)}, u32[]{:S(2)}, u32[]{:S(2)}) collective-permute-start(bf16[16,128,128]{2,1,0:T(8,128)(2,1)S(1)} %collective-permute-done.12.refs_10_), channel_id=1, source_target_pairs={{24,28},{26,30},{28,24},{30,26},{25,29},{27,31},{29,25},{31,27}} | collective-permute-start | bytes 1572872 | tf_op jit(solution)/shard_map/ppermute | solution.py:115
  57.2 14.9 %copy-start.1 = (bf16[64,128,128]{2,1,0:T(8,128)(2,1)}, bf16[64,128,128]{2,1,0:T(8,128)(2,1)S(1)}, u32[]{:S(2)}) copy-start(bf16[64,128,128]{2,1,0:T(8,128)(2,1)S(1)} %collective-permute-done.1.other_hbm) | copy-start | bytes 6291460
  72.1 12.3 %collective-permute-start.16 = (f32[2,4,128,128]{3,2,1,0:T(8,128)S(1)}, f32[2,4,128,128]{3,2,1,0:T(8,128)S(1)}, u32[]{:S(2)}, u32[]{:S(2)}) collective-permute-start(f32[2,4,128,128]{3,2,1,0:T(8,128)S(1)} %get-tuple-element.24), channel_id=1, source_target_pairs={{0,1},{1,0},{2,3},{3,2},{4,5},{5,4},{6,7},{7,6},{8,9},{9,8},{10,11... | collective-permute-start | bytes 1572872 | tf_op jit(solution)/shard_map/ppermute | solution.py:369
  84.6 1.6 collective-permute-start.17
  87.2 1.4 collective-permute-start.18
  88.6 5.6 %collective-permute-start.19 = (f32[128,256]{1,0:T(8,128)S(1)}, f32[128,256]{1,0:T(8,128)S(1)}, u32[]{:S(2)}, u32[]{:S(2)}) collective-permute-start(f32[128,256]{1,0:T(8,128)S(1)} %dynamic-slice_add_fusion.1), channel_id=1, source_target_pairs={{0,1},{1,0},{2,3},{3,2},{4,5},{5,4},{6,7},{7,6},{8,9},{9,8},{10,11... | collective-permute-start | bytes 393224 | tf_op jit(solution)/shard_map/ppermute | solution.py:357
  94.3 43.8 %copy-start.2 = (bf16[64,128,128]{2,1,0:T(8,128)(2,1)S(1)}, bf16[64,128,128]{2,1,0:T(8,128)(2,1)}, u32[]{:S(2)}) copy-start(bf16[64,128,128]{2,1,0:T(8,128)(2,1)} %copy-done.1) | copy-start | bytes 6291460
  94.3 5.0 %collective-permute-start.20 = (f32[128,256]{1,0:T(8,128)S(1)}, f32[128,256]{1,0:T(8,128)S(1)}, u32[]{:S(2)}, u32[]{:S(2)}) collective-permute-start(f32[128,256]{1,0:T(8,128)S(1)} %add.104), channel_id=1, source_target_pairs={{0,4},{2,6},{4,0},{6,2},{8,12},{10,14},{12,8},{14,10},{16,20},{18,... | collective-permute-start | bytes 393224 | tf_op jit(solution)/shard_map/ppermute | solution.py:358
  99.3 5.8 %collective-permute-start.21 = (f32[128,256]{1,0:T(8,128)S(1)}, f32[128,256]{1,0:T(8,128)S(1)}, u32[]{:S(2)}, u32[]{:S(2)}) collective-permute-start(f32[128,256]{1,0:T(8,128)S(1)} %add.105), channel_id=1, source_target_pairs={{0,8},{2,10},{4,12},{6,14},{8,0},{10,2},{12,4},{14,6},{16,24},{18,... | collective-permute-start | bytes 393224 | tf_op jit(solution)/shard_map/ppermute | solution.py:361
  105.2 10.0 %collective-permute-start.22 = (f32[128,256]{1,0:T(8,128)S(1)}, f32[128,256]{1,0:T(8,128)S(1)}, u32[]{:S(2)}, u32[]{:S(2)}) collective-permute-start(f32[128,256]{1,0:T(8,128)S(1)} %add.106), channel_id=1, source_target_pairs={{0,16},{2,18},{4,20},{6,22},{8,24},{10,26},{12,28},{14,30},{16,0},... | collective-permute-start | bytes 393224 | tf_op jit(solution)/shard_map/ppermute | solution.py:361
  115.2 1.4 collective-permute-start.23
  128.2 1.4 collective-permute-start.24
  129.7 8.4 %collective-permute-start.25 = (bf16[2,128,512]{2,1,0:T(8,128)(2,1)S(1)}, bf16[2,128,512]{2,1,0:T(8,128)(2,1)S(1)}, u32[]{:S(2)}, u32[]{:S(2)}) collective-permute-start(bf16[2,128,512]{2,1,0:T(8,128)(2,1)S(1)} %pad_maximum_fusion.1.near_hbm), channel_id=1, source_target_pairs={{0,1},{1,0},{2,3},{3,2},{4,5},{5,4},{6,7},{7,6},{8,9},{9,8},{10,11... | collective-permute-start | bytes 786440 | tf_op jit(solution)/shard_map/ppermute | solution.py:401
  145.1 16.7 %collective-permute-start.29 = (bf16[16,128,128]{2,1,0:T(8,128)(2,1)S(1)}, bf16[16,128,128]{2,1,0:T(8,128)(2,1)S(1)}, u32[]{:S(2)}, u32[]{:S(2)}) collective-permute-start(bf16[16,128,128]{2,1,0:T(8,128)(2,1)S(1)} %get-tuple-element.33), channel_id=1, source_target_pairs={{0,4},{2,6},{4,0},{6,2},{1,5},{3,7},{5,1},{7,3}} | collective-permute-start | bytes 1572872 | tf_op jit(solution)/shard_map/ppermute | solution.py:337
  148.5 15.5 %collective-permute-start.35 = (bf16[16,128,128]{2,1,0:T(8,128)(2,1)S(1)}, bf16[16,128,128]{2,1,0:T(8,128)(2,1)S(1)}, u32[]{:S(2)}, u32[]{:S(2)}) collective-permute-start(bf16[16,128,128]{2,1,0:T(8,128)(2,1)S(1)} %get-tuple-element.39), channel_id=1, source_target_pairs={{24,28},{26,30},{28,24},{30,26},{25,29},{27,31},{29,25},{31,27}} | collective-permute-start | bytes 1572872 | tf_op jit(solution)/shard_map/ppermute | solution.py:337
  149.2 23.8 %collective-permute-start.28 = (bf16[16,128,128]{2,1,0:T(8,128)(2,1)S(1)}, bf16[16,128,128]{2,1,0:T(8,128)(2,1)S(1)}, u32[]{:S(2)}, u32[]{:S(2)}) collective-permute-start(bf16[16,128,128]{2,1,0:T(8,128)(2,1)S(1)} %get-tuple-element.31), channel_id=1, source_target_pairs={{0,4},{2,6},{4,0},{6,2},{8,12},{10,14},{12,8},{14,10},{1,5},{3,7},... | collective-permute-start | bytes 1572872 | tf_op jit(solution)/shard_map/ppermute | solution.py:337
  161.9 11.8 %collective-permute-start.30 = (bf16[16,128,128]{2,1,0:T(8,128)(2,1)S(1)}, bf16[16,128,128]{2,1,0:T(8,128)(2,1)S(1)}, u32[]{:S(2)}, u32[]{:S(2)}) collective-permute-start(bf16[16,128,128]{2,1,0:T(8,128)(2,1)S(1)} %add_convert_fusion.6), channel_id=1, source_target_pairs={{0,8},{2,10},{4,12},{6,14},{1,9},{3,11},{5,13},{7,15}} | collective-permute-start | bytes 1572872 | tf_op jit(solution)/shard_map/ppermute | solution.py:341
  163.2 13.0 %collective-permute-start.34 = (bf16[16,128,128]{2,1,0:T(8,128)(2,1)S(1)}, bf16[16,128,128]{2,1,0:T(8,128)(2,1)S(1)}, u32[]{:S(2)}, u32[]{:S(2)}) collective-permute-start(bf16[16,128,128]{2,1,0:T(8,128)(2,1)S(1)} %get-tuple-element.37), channel_id=1, source_target_pairs={{16,20},{18,22},{20,16},{22,18},{24,28},{26,30},{28,24},{30,26},{1... | collective-permute-start | bytes 1572872 | tf_op jit(solution)/shard_map/ppermute | solution.py:337
  164.1 12.1 %collective-permute-start.36 = (bf16[16,128,128]{2,1,0:T(8,128)(2,1)S(1)}, bf16[16,128,128]{2,1,0:T(8,128)(2,1)S(1)}, u32[]{:S(2)}, u32[]{:S(2)}) collective-permute-start(bf16[16,128,128]{2,1,0:T(8,128)(2,1)S(1)} %add_convert_fusion.3), channel_id=1, source_target_pairs={{24,16},{26,18},{28,20},{30,22},{25,17},{27,19},{29,21},{31,23}} | collective-permute-start | bytes 1572872 | tf_op jit(solution)/shard_map/ppermute | solution.py:341
  164.8 19.4 %collective-permute-start.27 = (bf16[16,128,128]{2,1,0:T(8,128)(2,1)S(1)}, bf16[16,128,128]{2,1,0:T(8,128)(2,1)S(1)}, u32[]{:S(2)}, u32[]{:S(2)}) collective-permute-start(bf16[16,128,128]{2,1,0:T(8,128)(2,1)S(1)} %get-tuple-element.29), channel_id=1, source_target_pairs={{0,4},{2,6},{4,0},{6,2},{8,12},{10,14},{12,8},{14,10},{16,20},{18,... | collective-permute-start | bytes 1572872 | tf_op jit(solution)/shard_map/ppermute | solution.py:337
  173.0 15.4 %collective-permute-start.33 = (bf16[16,128,128]{2,1,0:T(8,128)(2,1)S(1)}, bf16[16,128,128]{2,1,0:T(8,128)(2,1)S(1)}, u32[]{:S(2)}, u32[]{:S(2)}) collective-permute-start(bf16[16,128,128]{2,1,0:T(8,128)(2,1)S(1)} %get-tuple-element.35), channel_id=1, source_target_pairs={{8,12},{10,14},{12,8},{14,10},{16,20},{18,22},{20,16},{22,18},{24,... | collective-permute-start | bytes 1572872 | tf_op jit(solution)/shard_map/ppermute | solution.py:337
  173.9 10.3 %collective-permute-start.31 = (bf16[16,128,128]{2,1,0:T(8,128)(2,1)S(1)}, bf16[16,128,128]{2,1,0:T(8,128)(2,1)S(1)}, u32[]{:S(2)}, u32[]{:S(2)}) collective-permute-start(bf16[16,128,128]{2,1,0:T(8,128)(2,1)S(1)} %add_convert_fusion.5), channel_id=1, source_target_pairs={{0,8},{2,10},{4,12},{6,14},{8,16},{10,18},{12,20},{14,22},{1,9},{3... | collective-permute-start | bytes 1572872 | tf_op jit(solution)/shard_map/ppermute | solution.py:341
  176.5 11.9 %collective-permute-start.37 = (bf16[16,128,128]{2,1,0:T(8,128)(2,1)S(1)}, bf16[16,128,128]{2,1,0:T(8,128)(2,1)S(1)}, u32[]{:S(2)}, u32[]{:S(2)}) collective-permute-start(bf16[16,128,128]{2,1,0:T(8,128)(2,1)S(1)} %add_convert_fusion.2), channel_id=1, source_target_pairs={{16,8},{18,10},{20,12},{22,14},{24,16},{26,18},{28,20},{30,22},{17... | collective-permute-start | bytes 1572872 | tf_op jit(solution)/shard_map/ppermute | solution.py:341
  177.2 16.6 %collective-permute-start.26 = (bf16[16,128,128]{2,1,0:T(8,128)(2,1)S(1)}, bf16[16,128,128]{2,1,0:T(8,128)(2,1)S(1)}, u32[]{:S(2)}, u32[]{:S(2)}) collective-permute-start(bf16[16,128,128]{2,1,0:T(8,128)(2,1)S(1)} %get-tuple-element.27), channel_id=1, source_target_pairs={{0,4},{2,6},{4,0},{6,2},{8,12},{10,14},{12,8},{14,10},{16,20},{18,... | collective-permute-start | bytes 1572872 | tf_op jit(solution)/shard_map/ppermute | solution.py:346
  184.4 10.6 %collective-permute-start.32 = (bf16[16,128,128]{2,1,0:T(8,128)(2,1)S(1)}, bf16[16,128,128]{2,1,0:T(8,128)(2,1)S(1)}, u32[]{:S(2)}, u32[]{:S(2)}) collective-permute-start(bf16[16,128,128]{2,1,0:T(8,128)(2,1)S(1)} %add_convert_fusion.4), channel_id=1, source_target_pairs={{0,8},{2,10},{4,12},{6,14},{8,16},{10,18},{12,20},{14,22},{16,24},... | collective-permute-start | bytes 1572872 | tf_op jit(solution)/shard_map/ppermute | solution.py:341
  188.6 11.1 %collective-permute-start.38 = (bf16[16,128,128]{2,1,0:T(8,128)(2,1)S(1)}, bf16[16,128,128]{2,1,0:T(8,128)(2,1)S(1)}, u32[]{:S(2)}, u32[]{:S(2)}) collective-permute-start(bf16[16,128,128]{2,1,0:T(8,128)(2,1)S(1)} %add_convert_fusion.1), channel_id=1, source_target_pairs={{8,0},{10,2},{12,4},{14,6},{16,8},{18,10},{20,12},{22,14},{24,16},... | collective-permute-start | bytes 1572872 | tf_op jit(solution)/shard_map/ppermute | solution.py:341
  199.9 11.9 %collective-permute-start.41 = (bf16[16,128,128]{2,1,0:T(8,128)(2,1)S(1)}, bf16[16,128,128]{2,1,0:T(8,128)(2,1)S(1)}, u32[]{:S(2)}, u32[]{:S(2)}) collective-permute-start(bf16[16,128,128]{2,1,0:T(8,128)(2,1)S(1)} %add_convert_fusion.refs_0_), channel_id=1, source_target_pairs={{8,0},{10,2},{12,4},{14,6},{16,8},{18,10},{20,12},{22,14},{24,16},... | collective-permute-start | bytes 1572872 | tf_op jit(solution)/shard_map/ppermute | solution.py:112
  201.2 11.8 %collective-permute-start.40 = (bf16[16,128,128]{2,1,0:T(8,128)(2,1)S(1)}, bf16[16,128,128]{2,1,0:T(8,128)(2,1)S(1)}, u32[]{:S(2)}, u32[]{:S(2)}) collective-permute-start(bf16[16,128,128]{2,1,0:T(8,128)(2,1)S(1)} %add_convert_fusion.refs_0_), channel_id=1, source_target_pairs={{0,8},{2,10},{4,12},{6,14},{8,16},{10,18},{12,20},{14,22},{16,24},... | collective-permute-start | bytes 1572872 | tf_op jit(solution)/shard_map/ppermute | solution.py:111
  211.8 12.6 %collective-permute-start.45 = (bf16[16,128,128]{2,1,0:T(8,128)(2,1)S(1)}, bf16[16,128,128]{2,1,0:T(8,128)(2,1)S(1)}, u32[]{:S(2)}, u32[]{:S(2)}) collective-permute-start(bf16[16,128,128]{2,1,0:T(8,128)(2,1)S(1)} %collective-permute-done.41.refs_3_), channel_id=1, source_target_pairs={{8,0},{10,2},{12,4},{14,6},{16,8},{18,10},{20,12},{22,14},{9,1},{1... | collective-permute-start | bytes 1572872 | tf_op jit(solution)/shard_map/ppermute | solution.py:112
  213.1 12.6 %collective-permute-start.44 = (bf16[16,128,128]{2,1,0:T(8,128)(2,1)S(1)}, bf16[16,128,128]{2,1,0:T(8,128)(2,1)S(1)}, u32[]{:S(2)}, u32[]{:S(2)}) collective-permute-start(bf16[16,128,128]{2,1,0:T(8,128)(2,1)S(1)} %collective-permute-done.40.refs_2_), channel_id=1, source_target_pairs={{8,16},{10,18},{12,20},{14,22},{16,24},{18,26},{20,28},{22,30},{9,... | collective-permute-start | bytes 1572872 | tf_op jit(solution)/shard_map/ppermute | solution.py:111
  213.8 14.9 %collective-permute-start.39 = (bf16[16,128,128]{2,1,0:T(8,128)(2,1)S(1)}, bf16[16,128,128]{2,1,0:T(8,128)(2,1)S(1)}, u32[]{:S(2)}, u32[]{:S(2)}) collective-permute-start(bf16[16,128,128]{2,1,0:T(8,128)(2,1)S(1)} %add_convert_fusion.refs_0_), channel_id=1, source_target_pairs={{0,4},{2,6},{4,0},{6,2},{8,12},{10,14},{12,8},{14,10},{16,20},{18,... | collective-permute-start | bytes 1572872 | tf_op jit(solution)/shard_map/ppermute | solution.py:108
  215.4 24.5 %collective-permute-start.43 = (bf16[16,128,128]{2,1,0:T(8,128)(2,1)S(1)}, bf16[16,128,128]{2,1,0:T(8,128)(2,1)S(1)}, u32[]{:S(2)}, u32[]{:S(2)}) collective-permute-start(bf16[16,128,128]{2,1,0:T(8,128)(2,1)S(1)} %collective-permute-done.41.refs_3_), channel_id=1, source_target_pairs={{0,4},{2,6},{4,0},{6,2},{8,12},{10,14},{12,8},{14,10},{16,20},{18,... | collective-permute-start | bytes 1572872 | tf_op jit(solution)/shard_map/ppermute | solution.py:116
  224.4 16.2 %collective-permute-start.49 = (bf16[16,128,128]{2,1,0:T(8,128)(2,1)S(1)}, bf16[16,128,128]{2,1,0:T(8,128)(2,1)S(1)}, u32[]{:S(2)}, u32[]{:S(2)}) collective-permute-start(bf16[16,128,128]{2,1,0:T(8,128)(2,1)S(1)} %collective-permute-done.45.refs_7_), channel_id=1, source_target_pairs={{8,0},{10,2},{12,4},{14,6},{9,1},{11,3},{13,5},{15,7}} | collective-permute-start | bytes 1572872 | tf_op jit(solution)/shard_map/ppermute | solution.py:112
  225.7 18.3 %collective-permute-start.48 = (bf16[16,128,128]{2,1,0:T(8,128)(2,1)S(1)}, bf16[16,128,128]{2,1,0:T(8,128)(2,1)S(1)}, u32[]{:S(2)}, u32[]{:S(2)}) collective-permute-start(bf16[16,128,128]{2,1,0:T(8,128)(2,1)S(1)} %collective-permute-done.44.refs_6_), channel_id=1, source_target_pairs={{16,24},{18,26},{20,28},{22,30},{17,25},{19,27},{21,29},{23,31}} | collective-permute-start | bytes 1572872 | tf_op jit(solution)/shard_map/ppermute | solution.py:111
  226.4 18.3 %collective-permute-start.42 = (bf16[16,128,128]{2,1,0:T(8,128)(2,1)S(1)}, bf16[16,128,128]{2,1,0:T(8,128)(2,1)S(1)}, u32[]{:S(2)}, u32[]{:S(2)}) collective-permute-start(bf16[16,128,128]{2,1,0:T(8,128)(2,1)S(1)} %collective-permute-done.40.refs_2_), channel_id=1, source_target_pairs={{8,12},{10,14},{12,8},{14,10},{16,20},{18,22},{20,16},{22,18},{24,... | collective-permute-start | bytes 1572872 | tf_op jit(solution)/shard_map/ppermute | solution.py:115
  228.7 21.6 %collective-permute-start.47 = (bf16[16,128,128]{2,1,0:T(8,128)(2,1)S(1)}, bf16[16,128,128]{2,1,0:T(8,128)(2,1)S(1)}, u32[]{:S(2)}, u32[]{:S(2)}) collective-permute-start(bf16[16,128,128]{2,1,0:T(8,128)(2,1)S(1)} %collective-permute-done.45.refs_7_), channel_id=1, source_target_pairs={{0,4},{2,6},{4,0},{6,2},{8,12},{10,14},{12,8},{14,10},{1,5},{3,7},... | collective-permute-start | bytes 1572872 | tf_op jit(solution)/shard_map/ppermute | solution.py:116
  239.9 10.3 %collective-permute-start.46 = (bf16[16,128,128]{2,1,0:T(8,128)(2,1)S(1)}, bf16[16,128,128]{2,1,0:T(8,128)(2,1)S(1)}, u32[]{:S(2)}, u32[]{:S(2)}) collective-permute-start(bf16[16,128,128]{2,1,0:T(8,128)(2,1)S(1)} %collective-permute-done.44.refs_6_), channel_id=1, source_target_pairs={{16,20},{18,22},{20,16},{22,18},{24,28},{26,30},{28,24},{30,26},{1... | collective-permute-start | bytes 1572872 | tf_op jit(solution)/shard_map/ppermute | solution.py:115
  240.6 15.2 %collective-permute-start.51 = (bf16[16,128,128]{2,1,0:T(8,128)(2,1)S(1)}, bf16[16,128,128]{2,1,0:T(8,128)(2,1)S(1)}, u32[]{:S(2)}, u32[]{:S(2)}) collective-permute-start(bf16[16,128,128]{2,1,0:T(8,128)(2,1)S(1)} %collective-permute-done.49.refs_11_), channel_id=1, source_target_pairs={{0,4},{2,6},{4,0},{6,2},{1,5},{3,7},{5,1},{7,3}} | collective-permute-start | bytes 1572872 | tf_op jit(solution)/shard_map/ppermute | solution.py:116
  244.1 11.8 %collective-permute-start.50 = (bf16[16,128,128]{2,1,0:T(8,128)(2,1)S(1)}, bf16[16,128,128]{2,1,0:T(8,128)(2,1)S(1)}, u32[]{:S(2)}, u32[]{:S(2)}) collective-permute-start(bf16[16,128,128]{2,1,0:T(8,128)(2,1)S(1)} %collective-permute-done.48.refs_10_), channel_id=1, source_target_pairs={{24,28},{26,30},{28,24},{30,26},{25,29},{27,31},{29,25},{31,27}} | collective-permute-start | bytes 1572872 | tf_op jit(solution)/shard_map/ppermute | solution.py:115
  262.7 9.2 %collective-permute-start.52 = (f32[2,4,128,128]{3,2,1,0:T(8,128)S(1)}, f32[2,4,128,128]{3,2,1,0:T(8,128)S(1)}, u32[]{:S(2)}, u32[]{:S(2)}) collective-permute-start(f32[2,4,128,128]{3,2,1,0:T(8,128)S(1)} %get-tuple-element.41), channel_id=1, source_target_pairs={{0,1},{1,0},{2,3},{3,2},{4,5},{5,4},{6,7},{7,6},{8,9},{9,8},{10,11... | collective-permute-start | bytes 1572872 | tf_op jit(solution)/shard_map/ppermute | solution.py:369
  272.0 1.6 collective-permute-start.53
  274.7 1.4 collective-permute-start.54
  276.1 5.6 %collective-permute-start.55 = (f32[128,256]{1,0:T(8,128)S(1)}, f32[128,256]{1,0:T(8,128)S(1)}, u32[]{:S(2)}, u32[]{:S(2)}) collective-permute-start(f32[128,256]{1,0:T(8,128)S(1)} %dynamic-slice_add_fusion), channel_id=1, source_target_pairs={{0,1},{1,0},{2,3},{3,2},{4,5},{5,4},{6,7},{7,6},{8,9},{9,8},{10,11... | collective-permute-start | bytes 393224 | tf_op jit(solution)/shard_map/ppermute | solution.py:357
  281.7 5.0 %collective-permute-start.56 = (f32[128,256]{1,0:T(8,128)S(1)}, f32[128,256]{1,0:T(8,128)S(1)}, u32[]{:S(2)}, u32[]{:S(2)}) collective-permute-start(f32[128,256]{1,0:T(8,128)S(1)} %add.123), channel_id=1, source_target_pairs={{0,4},{2,6},{4,0},{6,2},{8,12},{10,14},{12,8},{14,10},{16,20},{18,... | collective-permute-start | bytes 393224 | tf_op jit(solution)/shard_map/ppermute | solution.py:358
  286.8 8.4 %collective-permute-start.57 = (f32[128,256]{1,0:T(8,128)S(1)}, f32[128,256]{1,0:T(8,128)S(1)}, u32[]{:S(2)}, u32[]{:S(2)}) collective-permute-start(f32[128,256]{1,0:T(8,128)S(1)} %add.124), channel_id=1, source_target_pairs={{0,8},{2,10},{4,12},{6,14},{8,0},{10,2},{12,4},{14,6},{16,24},{18,... | collective-permute-start | bytes 393224 | tf_op jit(solution)/shard_map/ppermute | solution.py:361
  295.2 6.1 %collective-permute-start.58 = (f32[128,256]{1,0:T(8,128)S(1)}, f32[128,256]{1,0:T(8,128)S(1)}, u32[]{:S(2)}, u32[]{:S(2)}) collective-permute-start(f32[128,256]{1,0:T(8,128)S(1)} %add.125), channel_id=1, source_target_pairs={{0,16},{2,18},{4,20},{6,22},{8,24},{10,26},{12,28},{14,30},{16,0},... | collective-permute-start | bytes 393224 | tf_op jit(solution)/shard_map/ppermute | solution.py:361
  301.3 1.4 collective-permute-start.59
